TPU v7x, 512 devices: a whole 4x4x16 slice. The times are simulated.
512 devices in a mesh: gx: 16 (over z_hi, y, core), gy: 32 (over z_lo, x).
Axes of the slice: x: 4, y: 4, z: 16 (z_hi: 2, z_lo: 8; z = z_hi * 8 + z_lo), core: 2. Of those that a mesh axis runs over, the one named last changes fastest.
Arguments:
- load: float32 [2, 512, 512, 128], P(None, 'gx', 'gy'), may hold values from -8 to 8
- zones: int32 [512, 512, 128], P('gx', 'gy'), may hold values from 0 to 7
- conductance: float32 [2, 8], replicated, may hold values from 0.2 to 1
- capacity: float32 [2, 8], replicated, may hold values from 0.5 to 2
- coupling: float32 [8], replicated, may hold values from 0.2 to 0.8
Outputs:
- solution: float32 [2, 512, 512, 128], P(None, 'gx', 'gy')
- residual: float32 [2, 512, 512, 128], P(None, 'gx', 'gy')
All inputs are finite; a program needn't handle non-finite values.
Results may differ from a plain program's by a relative error of at most 0.006.
Values sent between devices are 32-bit elements; how exact they have to be, the bound alone decides.
A program may use at most 64 MiB of HBM per device.

v0:
```python
import jax
import jax.numpy as jnp
from jax import lax
from jax.sharding import PartitionSpec as P

BOX = 16
ITERS = 2


NEIGHBOURS = ((1, 0, 0), (-1, 0, 0), (0, 1, 0), (0, -1, 0), (0, 0, 1), (0, 0, -1))


def with_halo(block, sides, width):
    for axis, dim in sides:
        count = lax.axis_size(axis)
        forward = [(i, i + 1) for i in range(count - 1)]
        backward = [(target, source) for source, target in forward]
        low = lax.ppermute(
            lax.slice_in_dim(block, block.shape[dim] - width, None, axis=dim), axis, forward
        )
        high = lax.ppermute(lax.slice_in_dim(block, 0, width, axis=dim), axis, backward)
        block = jnp.concatenate([low, block, high], axis=dim)
    return block


def neighbour(array, offset_x, offset_y, offset_z):
    size_x, size_y, size_z = array.shape[-3:]
    return array[
        ...,
        1 + offset_x : size_x - 1 + offset_x,
        1 + offset_y : size_y - 1 + offset_y,
        1 + offset_z : size_z - 1 + offset_z,
    ]


def apply_operator(field, padded, kpadded, inside, mass):
    center = kpadded[:, 1:-1, 1:-1, 1:-1]
    flux = jnp.zeros_like(field)
    for offset_x, offset_y, offset_z in NEIGHBOURS:
        other_k = neighbour(kpadded, offset_x, offset_y, offset_z)
        other_in = neighbour(inside, offset_x, offset_y, offset_z)
        face = 0.5 * (center + jnp.where(other_in[None], other_k, center))
        flux = flux + face * (field - neighbour(padded, offset_x, offset_y, offset_z))
    first = mass[0] * field[0] + mass[2] * field[1] + flux[0]
    second = mass[2] * field[0] + mass[1] * field[1] + flux[1]
    return jnp.stack([first, second])


def box_matrix(cells):
    span = BOX + 2
    count = cells // BOX
    rows = jnp.arange(count * span)
    block_of = rows // span
    mode_of = rows % span
    columns = jnp.arange(cells + 2)
    offset = columns[None, :] - BOX * block_of[:, None]
    valid = (offset >= 0) & (offset < span)
    angle_arg = (
        jnp.pi
        * (offset + 1).astype(jnp.float32)
        * (mode_of[:, None] + 1).astype(jnp.float32)
        / (span + 1)
    )
    basis = jnp.sqrt(2.0 / (span + 1)) * jnp.sin(angle_arg)
    return jnp.where(valid, basis, 0.0)


def box_eigen():
    span = BOX + 2
    modes = jnp.arange(span).astype(jnp.float32)
    return 4.0 * jnp.sin(jnp.pi * (modes + 1.0) / (2.0 * (span + 1))) ** 2


def box_means(values):
    fields, size_x, size_y, size_z = values.shape
    shaped = values.reshape(fields, size_x // BOX, BOX, size_y // BOX, BOX, size_z // BOX, BOX)
    return jnp.mean(shaped, axis=(2, 4, 6))


def solve_boxes(padded, cbar, kbar):
    highest = lax.Precision.HIGHEST
    fields, length_x, length_y, length_z = padded.shape
    matrix_x = box_matrix(length_x - 2)
    matrix_y = box_matrix(length_y - 2)
    matrix_z = box_matrix(length_z - 2)
    spectral = jnp.einsum("am,fmyz->fayz", matrix_x, padded, precision=highest)
    spectral = jnp.einsum("bn,fanz->fabz", matrix_y, spectral, precision=highest)
    spectral = jnp.einsum("co,fabo->fabc", matrix_z, spectral, precision=highest)
    boxes_x, boxes_y, boxes_z = cbar.shape[1:]
    span = BOX + 2
    eigen = box_eigen()
    summed = eigen[:, None, None] + eigen[None, :, None] + eigen[None, None, :]
    divisor = (
        cbar[:, :, None, :, None, :, None]
        + kbar[:, :, None, :, None, :, None] * summed[None, None, :, None, :, None, :]
    )
    spectral = spectral.reshape(fields, boxes_x, span, boxes_y, span, boxes_z, span) / divisor
    spectral = spectral.reshape(fields, boxes_x * span, boxes_y * span, boxes_z * span)
    spectral = jnp.einsum("co,fabc->fabo", matrix_z, spectral, precision=highest)
    spectral = jnp.einsum("bn,fabo->fano", matrix_y, spectral, precision=highest)
    return jnp.einsum("am,fano->fmno", matrix_x, spectral, precision=highest)


def gather_rims(extended):
    size_x = extended.shape[1] - 2
    size_y = extended.shape[2] - 2
    edges = jnp.concatenate([extended[:, 0:1], extended[:, -1:]], axis=1)
    arrived = with_halo(edges, (("gx", 1),), 1)
    middle = extended[:, 1:-1]
    middle = middle.at[:, 0].add(arrived[:, 0]).at[:, size_x - 1].add(arrived[:, 3])
    edges = jnp.concatenate([middle[:, :, 0:1], middle[:, :, -1:]], axis=2)
    arrived = with_halo(edges, (("gy", 2),), 1)
    result = middle[:, :, 1:-1]
    return result.at[:, :, 0].add(arrived[:, :, 0]).at[:, :, size_y - 1].add(arrived[:, :, 3])


def shards(load, zones, conductance, capacity, coupling):
    cross = coupling * jnp.sqrt(capacity[0] * capacity[1])
    tables = jnp.concatenate([conductance, capacity, cross[None]], axis=0)
    marks = with_halo(zones + 1, (("gx", 0), ("gy", 1)), 1)
    marks = jnp.pad(marks, ((0, 0), (0, 0), (1, 1)))
    inside = marks > 0
    labels = jnp.arange(1, tables.shape[1] + 1, dtype=jnp.int32)
    indicator = (marks[None] == labels[:, None, None, None]).astype(jnp.float32)
    coeffs = jnp.einsum("tq,qxyz->txyz", tables, indicator, precision=lax.Precision.HIGHEST)
    kpadded = coeffs[0:2]
    mass = coeffs[2:5, 1:-1, 1:-1, 1:-1]
    cbar = box_means(mass[0:2])
    kbar = box_means(kpadded[:, 1:-1, 1:-1, 1:-1])
    solution = jnp.zeros_like(load)
    residual = load
    direction = load
    previous = jnp.float32(1.0)
    for iteration in range(ITERS):
        padded = with_halo(residual, (("gx", 1), ("gy", 2)), 1)
        padded = jnp.pad(padded, ((0, 0), (0, 0), (0, 0), (1, 1)))
        extended = solve_boxes(padded, cbar, kbar)[..., 1:-1]
        precond = gather_rims(extended)
        product = lax.psum(jnp.sum(residual * precond), ("gx", "gy"))
        if iteration == 0:
            direction = precond
        else:
            direction = precond + product / previous * direction
        operate_padded = with_halo(direction, (("gx", 1), ("gy", 2)), 1)
        operate_padded = jnp.pad(operate_padded, ((0, 0), (0, 0), (0, 0), (1, 1)))
        image = apply_operator(direction, operate_padded, kpadded, inside, mass)
        curvature = lax.psum(jnp.sum(direction * image), ("gx", "gy"))
        alpha = product / curvature
        solution = solution + alpha * direction
        residual = residual - alpha * image
        previous = product
    return (solution, residual)


def solution(mesh):
    in_specs = (P(None, "gx", "gy", None), P("gx", "gy", None), P(), P(), P())
    out_specs = (P(None, "gx", "gy", None), P(None, "gx", "gy", None))
    return jax.shard_map(shards, mesh=mesh, in_specs=in_specs, out_specs=out_specs, check_vma=False)
```

profile of v0, /device:TPU:1, one launch (start us, length us, event | category | flops | bytes accessed | tf_op | source)
XLA Modules:
  0.0 604.9 jit_solution(2671928480106741347)
XLA Ops:
  1.4 8.8 %collective-permute-start.1 = (f32[2,1,16,128]{3,1,2,0:T(1,128)S(1)}, f32[2,1,16,128]{3,1,2,0:T(1,128)S(1)}, u32[]{:S(2)}, u32[]{:S(2)}) collective-permute-start(f32[2,1,16,128]{3,1,2,0:T(1,128)S(1)} %bitcast.109), channel_id=1, source_target_pairs={{32,0},{64,32},{96,64},{128,96},{160,128},{192,160},{224,192},{256... | collective-permute-start | bytes 49160 | tf_op jit(solution)/shard_map/ppermute | solution.py:21
  10.2 1.9 collective-permute-start
  13.8 1.9 collective-permute-start.4
  15.7 2.4 collective-permute-start.5
  19.2 2.0 copy.24
  25.8 4.0 collective-permute-start.2
  31.7 2.4 fusion
  34.1 2.2 copy-done
  38.6 2.0 fusion.31
  40.6 2.0 fusion.10
  42.6 2.1 fusion.6
  44.8 2.5 fusion.14
  51.9 3.7 collective-permute-start.8
  56.3 1.9 collective-permute-start.9
  58.3 3.0 collective-permute-done.9
  61.4 4.3 collective-permute-start.10
  67.1 3.3 collective-permute-done.11
  70.5 3.4 collective-permute-start.13
  73.8 1.9 collective-permute-start.12
  76.1 6.3 %collective-permute-done.12 = f32[2,1,16,128]{3,0,2,1:T(2,128)S(1)} collective-permute-done((f32[2,1,16,128]{3,0,2,1:T(2,128)S(1)}, f32[2,1,16,128]{3,0,2,1:T(2,128)S(1)}, u32[]{:S(2)}, u32[]{:S(2)}) %collective-permute-start.12) | collective-permute-done | bytes 16416 | tf_op jit(solution)/shard_map/ppermute | solution.py:21
  82.4 3.5 collective-permute-start.15
  88.1 5.0 collective-permute-done.14
  93.0 3.3 select_maximum_fusion.14
  96.4 7.2 %fusion.66 = f32[2,32,16,128]{3,0,2,1:T(2,128)S(1)} fusion(f32[2,32,16,128]{3,0,2,1:T(2,128)S(1)} %fusion.89, f32[2,34,18,130]{3,0,2,1:T(2,128)S(1)} %select_maximum_fusion.14, f32[2,34,1,128]{3,0,2,1:T(2,128)S(1)} %collective-permute-done.15, f32[2,1,16,128]{3,0,2,1:T(2,128)S(1)} %collective-permute-done.12, ...), kind=kLoop, calls=%fused_computation.101 | loop fusion | flops 5636096 | bytes 6262784 | tf_op jit(solution)/shard_map/add | solution.py:43
  107.2 151.7 %all-reduce.5 = (f32[]{:T(128)}, f32[]{:T(128)}) all-reduce(f32[]{:T(128)} %get-tuple-element.107, f32[]{:T(128)} %get-tuple-element.106), channel_id=1, replica_groups=mesh['gx'=16,'gy'=32] {'gx','gy'}, use_global_device_ids=true, to_apply=%region_5.6 | all-reduce | flops 2 | bytes 16 | tf_op jit(solution)/shard_map/psum | solution.py:139
  261.1 1.9 collective-permute-start.16
  263.0 2.5 collective-permute-start.17
  265.5 2.6 collective-permute-done.17
  268.1 2.4 collective-permute-start.18
  272.0 3.2 collective-permute-done.19
  277.2 2.0 fusion.8
  279.2 2.0 fusion.4
  281.3 2.2 fusion.12
  288.3 3.4 collective-permute-start.20
  292.4 1.9 collective-permute-start.21
  294.4 3.0 collective-permute-done.21
  297.5 3.1 collective-permute-start.22
  302.0 3.5 collective-permute-done.23
  307.0 133.3 %psum.30 = f32[]{:T(128)} all-reduce(f32[]{:T(128)} %multiply_reduce_fusion.1), channel_id=1, replica_groups=mesh['gx'=16,'gy'=32] {'gx','gy'}, use_global_device_ids=true, to_apply=%region_9.10 | all-reduce | flops 1 | bytes 8 | tf_op jit(solution)/shard_map/psum | solution.py:139
  441.7 1.9 collective-permute-start.25
  443.6 2.4 collective-permute-start.24
  446.1 2.6 collective-permute-done.24
  448.7 2.4 collective-permute-start.27
  452.4 3.4 collective-permute-done.26
  455.8 3.3 select_maximum_fusion.10
  459.1 12.5 %fusion.51 = f32[2,32,16,128]{3,0,2,1:T(2,128)S(1)} fusion(f32[2,32,16,128]{3,0,2,1:T(2,128)S(1)} %bitcast.97, f32[2,34,18,130]{3,0,2,1:T(2,128)S(1)} %select_maximum_fusion.10, f32[2,34,1,128]{3,0,2,1:T(2,128)S(1)} %collective-permute-done.27, f32[2,1,16,128]{3,0,2,1:T(2,128)S(1)} %collective-permute-done.24, ...), kind=kLoop, calls=%fused_computation.76 | loop fusion | flops 5636096 | bytes 6262784 | tf_op jit(solution)/shard_map/add | solution.py:43
  471.6 6.8 %slice_add_fusion.1 = (f32[1,32,16,128]{3,0,2,1:T(1,128)S(1)}, f32[1,32,16,128]{3,0,2,1:T(1,128)S(1)}) fusion(f32[2,32,16,128]{3,0,2,1:T(2,128)S(1)} %fusion.51, f32[2,32,16,128]{3,0,2,1:T(2,128)S(1)} %bitcast.98, f32[5,34,18,130]{3,0,2,1:T(8,128)} %copy-done), kind=kLoop, calls=%fused_computation.138 | loop fusion | flops 524288 | bytes 2359296 | tf_op jit(solution)/shard_map/add | solution.py:44
  479.5 120.7 %psum.31 = f32[]{:T(128)} all-reduce(f32[]{:T(128)} %multiply_reduce_fusion), channel_id=1, replica_groups=mesh['gx'=16,'gy'=32] {'gx','gy'}, use_global_device_ids=true, to_apply=%region_11.12 | all-reduce | flops 1 | bytes 8 | tf_op jit(solution)/shard_map/psum | solution.py:147
  (124 shorter events, 43.3 us)
Async XLA Ops:
  1.4 24.4 %collective-permute-start.1 = (f32[2,1,16,128]{3,1,2,0:T(1,128)S(1)}, f32[2,1,16,128]{3,1,2,0:T(1,128)S(1)}, u32[]{:S(2)}, u32[]{:S(2)}) collective-permute-start(f32[2,1,16,128]{3,1,2,0:T(1,128)S(1)} %bitcast.109), channel_id=1, source_target_pairs={{32,0},{64,32},{96,64},{128,96},{160,128},{192,160},{224,192},{256... | collective-permute-start | bytes 49160 | tf_op jit(solution)/shard_map/ppermute | solution.py:21
  10.2 15.6 %collective-permute-start = (f32[2,1,16,128]{3,1,2,0:T(1,128)S(1)}, f32[2,1,16,128]{3,1,2,0:T(1,128)S(1)}, u32[]{:S(2)}, u32[]{:S(2)}) collective-permute-start(f32[2,1,16,128]{3,1,2,0:T(1,128)S(1)} %bitcast.108), channel_id=1, source_target_pairs={{0,32},{32,64},{64,96},{96,128},{128,160},{160,192},{192,224},{224... | collective-permute-start | bytes 49160 | tf_op jit(solution)/shard_map/ppermute | solution.py:18
  13.1 0.7 copy-start.2
  13.8 8.7 %collective-permute-start.4 = (s32[1,16,128]{2,1,0:T(8,128)S(1)}, s32[1,16,128]{2,1,0:T(8,128)S(1)}, u32[]{:S(2)}, u32[]{:S(2)}) collective-permute-start(s32[1,16,128]{2,1,0:T(8,128)S(1)} %get-tuple-element.140), channel_id=1, source_target_pairs={{0,32},{32,64},{64,96},{96,128},{128,160},{160,192},{192,224},{224... | collective-permute-start | bytes 24584 | tf_op jit(solution)/shard_map/ppermute | solution.py:18
  15.7 6.8 %collective-permute-start.5 = (s32[1,16,128]{2,1,0:T(8,128)S(1)}, s32[1,16,128]{2,1,0:T(8,128)S(1)}, u32[]{:S(2)}, u32[]{:S(2)}) collective-permute-start(s32[1,16,128]{2,1,0:T(8,128)S(1)} %get-tuple-element.141), channel_id=1, source_target_pairs={{32,0},{64,32},{96,64},{128,96},{160,128},{192,160},{224,192},{256... | collective-permute-start | bytes 24584 | tf_op jit(solution)/shard_map/ppermute | solution.py:21
  22.2 1.0 copy-start.3
  22.2 3.6 copy-start.4
  22.4 22.3 %copy-start.5 = (f32[36,18,144]{2,1,0:T(8,128)}, f32[36,18,144]{2,1,0:T(8,128)S(1)}, u32[]{:S(2)}) copy-start(f32[36,18,144]{2,1,0:T(8,128)S(1)} %copy.30) | copy-start | bytes 1119748
  22.4 9.2 %copy-start.7 = (f32[2,8]{1,0:T(2,128)S(1)}, f32[2,8]{1,0:T(2,128)}, u32[]{:S(2)}) copy-start(f32[2,8]{1,0:T(2,128)} %param.24) | copy-start | bytes 196
  22.5 9.2 %copy-start.8 = (f32[2,8]{1,0:T(2,128)S(1)}, f32[2,8]{1,0:T(2,128)}, u32[]{:S(2)}) copy-start(f32[2,8]{1,0:T(2,128)} %param.23) | copy-start | bytes 196
  23.2 8.1 %collective-permute-start.6 = (s32[34,1,128]{2,1,0:T(1,128)S(1)}, s32[34,1,128]{2,1,0:T(1,128)S(1)}, u32[]{:S(2)}, u32[]{:S(2)}) collective-permute-start(s32[34,1,128]{2,1,0:T(1,128)S(1)} %get-tuple-element.138), channel_id=1, source_target_pairs={{0,1},{1,2},{2,3},{3,4},{4,5},{5,6},{6,7},{7,8},{8,9},{9,10},{10,1... | collective-permute-start | bytes 52232 | tf_op jit(solution)/shard_map/ppermute | solution.py:18
  24.5 6.8 %collective-permute-start.7 = (s32[34,1,128]{2,1,0:T(1,128)S(1)}, s32[34,1,128]{2,1,0:T(1,128)S(1)}, u32[]{:S(2)}, u32[]{:S(2)}) collective-permute-start(s32[34,1,128]{2,1,0:T(1,128)S(1)} %get-tuple-element.139), channel_id=1, source_target_pairs={{1,0},{2,1},{3,2},{4,3},{5,4},{6,5},{7,6},{8,7},{9,8},{10,9},{11,1... | collective-permute-start | bytes 52232 | tf_op jit(solution)/shard_map/ppermute | solution.py:21
  25.8 12.8 %collective-permute-start.2 = (f32[2,34,1,128]{3,1,2,0:T(8,128)S(1)}, f32[2,34,1,128]{3,1,2,0:T(8,128)S(1)}, u32[]{:S(2)}, u32[]{:S(2)}) collective-permute-start(f32[2,34,1,128]{3,1,2,0:T(8,128)S(1)} %get-tuple-element.128), channel_id=1, source_target_pairs={{0,1},{1,2},{2,3},{3,4},{4,5},{5,6},{6,7},{7,8},{8,9},{9,10},{10,1... | collective-permute-start | bytes 104456 | tf_op jit(solution)/shard_map/ppermute | solution.py:18
  29.8 8.8 %collective-permute-start.3 = (f32[2,34,1,128]{3,1,2,0:T(8,128)S(1)}, f32[2,34,1,128]{3,1,2,0:T(8,128)S(1)}, u32[]{:S(2)}, u32[]{:S(2)}) collective-permute-start(f32[2,34,1,128]{3,1,2,0:T(8,128)S(1)} %get-tuple-element.129), channel_id=1, source_target_pairs={{1,0},{2,1},{3,2},{4,3},{5,4},{6,5},{7,6},{8,7},{9,8},{10,9},{11,1... | collective-permute-start | bytes 104456 | tf_op jit(solution)/shard_map/ppermute | solution.py:21
  34.1 2.2 copy-start
  47.2 49.1 %slice-start = ((s8[5013504]{0:T(1024)(128)(4,1)}), s8[4194304]{0:T(1024)(128)(4,1)S(1)}, s32[]{:S(2)}) async-start(s8[5013504]{0:T(1024)(128)(4,1)} %bitcast.91), calls=%async_computation | async-start | bytes 8388608
  50.8 45.6 %slice-start.1 = ((s8[5013504]{0:T(1024)(128)(4,1)}), s8[819200]{0:T(1024)(128)(4,1)S(1)}, s32[]{:S(2)}) async-start(s8[5013504]{0:T(1024)(128)(4,1)} %bitcast.91), calls=%async_computation.1 | async-start | bytes 1638400
  51.9 6.3 %collective-permute-start.8 = (f32[2,1,18,128]{3,0,2,1:T(2,128)S(1)}, f32[2,1,18,128]{3,0,2,1:T(2,128)S(1)}, u32[]{:S(2)}, u32[]{:S(2)}) collective-permute-start(f32[2,1,18,128]{3,0,2,1:T(2,128)S(1)} %get-tuple-element.117), channel_id=1, source_target_pairs={{0,32},{32,64},{64,96},{96,128},{128,160},{160,192},{192,224},{224... | collective-permute-start | bytes 55304 | tf_op jit(solution)/shard_map/ppermute | solution.py:18
  56.3 5.1 collective-permute-start.9
  61.4 5.6 collective-permute-start.10
  65.8 4.7 collective-permute-start.11
  70.5 5.6 collective-permute-start.13
  73.8 8.5 %collective-permute-start.12 = (f32[2,1,16,128]{3,0,2,1:T(2,128)S(1)}, f32[2,1,16,128]{3,0,2,1:T(2,128)S(1)}, u32[]{:S(2)}, u32[]{:S(2)}) collective-permute-start(f32[2,1,16,128]{3,0,2,1:T(2,128)S(1)} %get-tuple-element.135), channel_id=1, source_target_pairs={{32,0},{64,32},{96,64},{128,96},{160,128},{192,160},{224,192},{256... | collective-permute-start | bytes 49160 | tf_op jit(solution)/shard_map/ppermute | solution.py:21
  82.4 5.6 collective-permute-start.15
  85.9 7.1 %collective-permute-start.14 = (f32[2,34,1,128]{3,0,2,1:T(2,128)S(1)}, f32[2,34,1,128]{3,0,2,1:T(2,128)S(1)}, u32[]{:S(2)}, u32[]{:S(2)}) collective-permute-start(f32[2,34,1,128]{3,0,2,1:T(2,128)S(1)} %get-tuple-element.127), channel_id=1, source_target_pairs={{1,0},{2,1},{3,2},{4,3},{5,4},{6,5},{7,6},{8,7},{9,8},{10,9},{11,1... | collective-permute-start | bytes 104456 | tf_op jit(solution)/shard_map/ppermute | solution.py:21
  103.6 1.9 copy-start.1
  261.1 4.4 collective-permute-start.16
  263.0 5.1 collective-permute-start.17
  268.1 3.9 collective-permute-start.18
  270.5 4.7 collective-permute-start.19
  279.2 2.1 copy-start.6
  288.3 6.0 collective-permute-start.20
  292.4 5.1 collective-permute-start.21
  297.5 4.5 collective-permute-start.22
  300.7 4.8 collective-permute-start.23
  441.7 4.4 collective-permute-start.25
  443.6 5.1 collective-permute-start.24
  448.7 3.7 collective-permute-start.27
  451.1 4.7 collective-permute-start.26
where the time goes:
time: 609 us; the launch traced here: 605 us
  blocking collectives  406 us (67%)
  starting transfers between devices  70.7 us (12%)
  other arithmetic  46.1 us (8%)
  waiting for transfers between devices  36 us (6%)
  matrix products  25.9 us (4%)
  local copies, waits for them, and re-layouts  14.6 us (2%)
    psum x2, blocking collectives, shards(): product = lax.psum(jnp.sum(residual * precond), ('gx', 'gy'))  285 us
    psum x1, blocking collectives, shards(): curvature = lax.psum(jnp.sum(direction * image), ('gx', 'gy'))  121 us
    ppermute x14, starting transfers between devices, with_halo(): lax.ppermute(lax.slice_in_dim(block, block.shape[dim] - width, None, axis...  39.1 us
    ppermute x14, waiting for transfers between devices, with_halo(): lax.ppermute(lax.slice_in_dim(block, 0, width, axis=dim), axis, backward)  35.9 us
    ppermute x14, starting transfers between devices, with_halo(): lax.ppermute(lax.slice_in_dim(block, 0, width, axis=dim), axis, backward)  31.6 us
    add x2, other arithmetic, apply_operator(): flux + face * (field - neighbour(padded, offset_x, offset_y, offset_z))  19.7 us
  transfers between devices with their start and end apart: 28, of which 10 were waited for; matrix products, arithmetic and copies ran while one was open for 2% of the time, Pallas kernels for 0%

commit v1 on v0

v1 whole, which is shorter than its diff:
```python
import functools

import jax
import jax.numpy as jnp
import numpy as np
from jax import lax
from jax.experimental import pallas as pl
from jax.experimental.pallas import tpu as pltpu
from jax.sharding import PartitionSpec as P

BOX = 16
SPAN = BOX + 2
BX = 32
BY = 16
NZ = 128
ZONES = 8
LX = BX + 4
PX = 40
MODES = 336
OWN = SPAN * BY
KIN = OWN + 48
MOUT = OWN + 144
F32 = jnp.float32
BF16 = jnp.bfloat16
MESH = pl.DeviceIdType.MESH


def split3(matrix):
    high = np.asarray(matrix, np.float32).astype(jnp.bfloat16)
    low = (np.asarray(matrix, np.float32) - high.astype(np.float32)).astype(jnp.bfloat16)
    return high, low


def constants():
    index = np.arange(SPAN)
    basis = np.sqrt(2.0 / (SPAN + 1)) * np.sin(np.pi * np.outer(index + 1, index + 1) / (SPAN + 1))
    lam = 4.0 * np.sin(np.pi * (index + 1) / (2.0 * (SPAN + 1))) ** 2
    forward = np.zeros((SPAN, SPAN, KIN))
    inner = np.einsum("ix,jy->ijxy", basis, basis[:, 1:17])
    forward[:, :, :OWN] = inner.reshape(SPAN, SPAN, OWN)
    for side, row in ((0, 0), (1, 17)):
        start = OWN + 24 * side + 1
        forward[:, :, start : start + SPAN] = np.einsum("ix,j->ijx", basis, basis[:, row])
    full = np.zeros((MODES, KIN))
    full[: SPAN * SPAN] = forward.reshape(SPAN * SPAN, KIN)
    high, low = split3(full)
    to_modes = np.concatenate([high, high, low], axis=1)
    inverse = np.zeros((MOUT, SPAN, SPAN))
    inverse[:OWN] = np.einsum("xi,yj->xyij", basis, basis[1:17]).reshape(OWN, SPAN, SPAN)
    for place, row in enumerate((0, 1, 2, 15, 16, 17)):
        start = OWN + 24 * place + 1
        inverse[start : start + SPAN] = np.einsum("xi,j->xij", basis, basis[row])
    full = np.zeros((MOUT, MODES))
    full[:, : SPAN * SPAN] = inverse.reshape(MOUT, SPAN * SPAN)
    high, low = split3(full)
    from_modes = np.concatenate([high, high, low], axis=1)
    boxes = NZ // BOX
    count = boxes * SPAN
    banded = np.zeros((NZ, count))
    for box in range(boxes):
        for offset in range(SPAN):
            cell = BOX * box + offset - 1
            if 0 <= cell < NZ:
                banded[cell, box * SPAN : (box + 1) * SPAN] = basis[:, offset]
    rest = count - 128
    lanes = np.concatenate([np.arange(128)] + [128 + np.arange(rest)] * 3)
    wide = np.zeros((NZ, 256))
    wide[:, : lanes.size] = banded[:, lanes]
    high, low = split3(wide)
    z_forward = np.concatenate([high, high, low], axis=0)
    high, low = split3(banded.T)
    tail = np.zeros((128, NZ), jnp.bfloat16)
    tail[:rest] = high[128:]
    tail[rest : 2 * rest] = high[128:]
    tail[2 * rest : 3 * rest] = low[128:]
    z_inverse = np.concatenate([high[:128], high[:128], low[:128], tail], axis=0)
    summed = np.zeros((MODES, 256), np.float32)
    plane = (lam[:, None] + lam[None, :]).reshape(-1)
    summed[: SPAN * SPAN, : lanes.size] = plane[:, None] + lam[lanes % SPAN][None, :]
    group = np.zeros((NZ, 256))
    group[:, : lanes.size] = (np.arange(NZ)[:, None] // BOX) == (lanes // SPAN)[None, :]
    group = np.concatenate([group] * 3, axis=0).astype(jnp.bfloat16)
    return to_modes, from_modes, z_forward, z_inverse, summed, group


def lookup(zone, table):
    bit0 = (zone & 1) != 0
    bit1 = (zone & 2) != 0
    bit2 = (zone & 4) != 0

    def pick(values):
        a = jnp.where(bit0, values[1], values[0])
        b = jnp.where(bit0, values[3], values[2])
        c = jnp.where(bit0, values[5], values[4])
        d = jnp.where(bit0, values[7], values[6])
        return jnp.where(bit2, jnp.where(bit1, d, c), jnp.where(bit1, b, a))

    return [pick(values) for values in table]


def halves(value):
    high = value.astype(BF16)
    low = (value - high.astype(F32)).astype(BF16)
    return high, low


def dot(a, b):
    return jnp.dot(a, b, preferred_element_type=F32)


def body(
    nx, ny,
    load_ref, zones_ref, cond_ref, cap_ref, coup_ref,
    tf_hbm, ti_hbm, zf_hbm, zi_hbm, lam_hbm, group_hbm,
    x_out, r_out,
    tf, ti, zf, zi, lam, group,
    r_own, r_pk, zone, zone_pk, zone_send, zone_recv,
    r_send, r_recv, r_corner_send, r_corner,
    k_own, k_pk, c_own, c_pk, cross, cross_pk,
    fx, fym, fyp, fzm, fzp, diag, diag_pk, dinv,
    u1, p1, v1, zp, q_own, q_pk, u2, p2, v2, wp, u_vec,
    xl1, xc1, xcs1, yr1, dg1, dgs1, xl2, xc2, xcs2, yr2, dg2, dgs2,
    ar1, ar2,
    local_sem, send_sem, recv_sem, ar_send, ar_recv,
):
    gx = lax.axis_index("gx")
    gy = lax.axis_index("gy")
    has = {"xm": gx > 0, "xp": gx < nx - 1, "ym": gy > 0, "yp": gy < ny - 1}
    ax, ay = min(8, nx // 2), min(4, ny // 2)
    plane, depth = ax * ay, (nx // ax) * (ny // ay)
    here = (gx % ax) * ay + gy % ay
    level = (gx // ax) * (ny // ay) + gy // ay

    def plane_id(k):
        t = (here + k) % plane
        return ((gx // ax) * ax + t // ay, (gy // ay) * ay + t % ay)

    def depth_id(k):
        t = (level + k) % depth
        return ((t // (ny // ay)) * ax + gx % ax, (t % (ny // ay)) * ay + gy % ay)

    sides = [
        ("xm", has["xm"], (gx - 1, gy)),
        ("xp", has["xp"], (gx + 1, gy)),
        ("ym", has["ym"], (gx, gy - 1)),
        ("yp", has["yp"], (gx, gy + 1)),
        ("mm", jnp.logical_and(has["xm"], has["ym"]), (gx - 1, gy - 1)),
        ("pp", jnp.logical_and(has["xp"], has["yp"]), (gx + 1, gy + 1)),
        ("mp", jnp.logical_and(has["xm"], has["yp"]), (gx - 1, gy + 1)),
        ("pm", jnp.logical_and(has["xp"], has["ym"]), (gx + 1, gy - 1)),
    ]

    loads = [
        pltpu.make_async_copy(load_ref.at[0], r_own.at[0, 2:34], local_sem.at[0]),
        pltpu.make_async_copy(load_ref.at[1], r_own.at[1, 2:34], local_sem.at[1]),
        pltpu.make_async_copy(zones_ref, zone.at[2:34], local_sem.at[2]),
    ]
    weights = [
        pltpu.make_async_copy(source, target, local_sem.at[3 + n])
        for n, (source, target) in enumerate(
            ((tf_hbm, tf), (zf_hbm, zf), (group_hbm, group), (lam_hbm, lam), (zi_hbm, zi), (ti_hbm, ti))
        )
    ]
    for copy in loads + weights:
        copy.start()

    barrier = pltpu.get_barrier_semaphore()
    for _, present, device in sides:

        @pl.when(present)
        def _():
            pl.semaphore_signal(barrier, inc=1, device_id=device, device_id_type=MESH)

    def greet_plane(k, carry):
        pl.semaphore_signal(barrier, inc=1, device_id=plane_id(k), device_id_type=MESH)
        return carry

    def greet_depth(k, carry):
        pl.semaphore_signal(barrier, inc=1, device_id=depth_id(k), device_id_type=MESH)
        return carry

    lax.fori_loop(1, plane, greet_plane, 0)
    lax.fori_loop(1, depth, greet_depth, 0)

    def clear(*refs):
        for ref in refs:
            ref[...] = jnp.zeros(ref.shape, ref.dtype)

    r_pk[...] = jnp.zeros(r_pk.shape, F32)
    for side, name in enumerate(("xm", "xp")):

        @pl.when(jnp.logical_not(has[name]))
        def _():
            clear(r_own.at[0, 1 + 33 * side], r_own.at[1, 1 + 33 * side])
            clear(xl1.at[side], xc1.at[side], xl2.at[side], xc2.at[side])

    for side, name in enumerate(("ym", "yp")):

        @pl.when(jnp.logical_not(has[name]))
        def _():
            clear(r_recv.at[side], yr1.at[side], yr2.at[side])

    for corner in range(4):

        @pl.when(jnp.logical_not(sides[4 + corner][1]))
        def _():
            clear(r_corner.at[corner], dg1.at[corner], dg2.at[corner])

    for copy in loads:
        copy.wait()

    for field in range(2):
        r_send[0, field] = r_own[field, 2:34, 0]
        r_send[1, field] = r_own[field, 2:34, BY - 1]
    for corner, (layer, row) in enumerate(((2, 0), (33, 15), (2, 15), (33, 0))):
        for field in range(2):
            r_corner_send[corner, field : field + 1] = r_own[field, layer, row : row + 1]

    members = jnp.int32(plane - 1 + depth - 1)
    for _, present, _ in sides:
        members = members + present.astype(jnp.int32)
    pl.semaphore_wait(barrier, members)

    def remote(number, source, target, slot):
        _, present, device = sides[number]
        return present, pltpu.make_async_remote_copy(
            src_ref=source,
            dst_ref=target,
            send_sem=send_sem.at[slot],
            recv_sem=recv_sem.at[slot],
            device_id=device,
            device_id_type=MESH,
        )

    def start(copies):
        for present, copy in copies:

            @pl.when(present)
            def _():
                copy.start()

    def finish_recv(copies, arrives):
        for (_, copy), number in zip(copies, arrives):

            @pl.when(sides[number][1])
            def _():
                copy.wait_recv()

    def finish_send(copies):
        for present, copy in copies:

            @pl.when(present)
            def _():
                copy.wait_send()

    first = [
        remote(0, r_own.at[:, 2], r_own.at[:, 34], 0),
        remote(1, r_own.at[:, 33], r_own.at[:, 1], 1),
        remote(2, r_send.at[0], r_recv.at[1], 2),
        remote(3, r_send.at[1], r_recv.at[0], 3),
        remote(4, r_corner_send.at[0], r_corner.at[1], 4),
        remote(5, r_corner_send.at[1], r_corner.at[0], 5),
        remote(6, r_corner_send.at[2], r_corner.at[3], 6),
        remote(7, r_corner_send.at[3], r_corner.at[2], 7),
    ]
    origin = [1, 0, 3, 2, 5, 4, 7, 6]
    start(first)
    zone_x = [
        remote(0, zone.at[2:4], zone.at[34:36], 8),
        remote(1, zone.at[32:34], zone.at[0:2], 9),
    ]
    start(zone_x)

    table = [[ref[f, q] for q in range(ZONES)] for ref in (cond_ref, cap_ref) for f in range(2)]
    table.append([coup_ref[q] for q in range(ZONES)])

    def own_coefficients(layer, sums):
        k0, k1, c0, c1, share = lookup(zone[layer], table)
        k_own[layer, 8:24] = k0
        k_own[LX + layer, 8:24] = k1
        c_own[0, layer] = c0
        c_own[1, layer] = c1
        cross[layer] = share * jnp.sqrt(c0 * c1)
        return tuple(s + v[:8] + v[8:] for s, v in zip(sums, (c0, c1, k0, k1)))

    zero = jnp.zeros((8, NZ), F32)
    pieces = []
    for box in range(2):
        sums = lax.fori_loop(2 + BOX * box, 2 + BOX * (box + 1), own_coefficients, (zero,) * 4)
        pieces.extend(jnp.sum(s, axis=0, keepdims=True) for s in sums)
    total = jnp.concatenate(pieces, axis=0)
    part0 = total.astype(BF16)
    rest = total - part0.astype(F32)
    part1 = rest.astype(BF16)
    part2 = (rest - part1.astype(F32)).astype(BF16)
    for copy in weights:
        copy.wait()
    means = dot(jnp.concatenate([part0, part1, part2], axis=1), group[...]) * (1.0 / BOX**3)
    lane = lax.broadcasted_iota(jnp.int32, (1, 256), 1)
    unused = jnp.where(lane >= 128 + 48, 1.0, 0.0)
    for box in range(2):
        for field in range(2):
            cbar = means[4 * box + field : 4 * box + field + 1] + unused
            kbar = means[4 * box + 2 + field : 4 * box + 3 + field]
            dinv[2 * box + field] = 1.0 / (cbar + kbar * lam[...])

    lane_tail = lax.broadcasted_iota(jnp.int32, (1, 128), 1)
    low_lanes = jnp.logical_and(lane_tail >= 16, lane_tail < 32)

    def apply_boxes(own, packed, out, out_pk):
        for box in range(2):
            columns = []
            for field in range(2):
                inner = own[field, 1 + BOX * box : 1 + BOX * box + SPAN].reshape(OWN, NZ)
                edge = [packed[side, field, BOX * box : BOX * box + 24] for side in range(2)]
                columns.append(jnp.concatenate([inner] + edge, axis=0))
            high, low = halves(jnp.concatenate(columns, axis=1))
            modes = dot(tf[...], jnp.concatenate([high, low, high], axis=0))
            columns = []
            for field in range(2):
                high, low = halves(modes[:, NZ * field : NZ * (field + 1)])
                deep = dot(jnp.concatenate([high, low, high], axis=1), zf[...])
                deep = deep * dinv[2 * box + field]
                high, low = halves(deep[:, :128])
                tail = deep[:, 128:]
                tail_high = tail.astype(BF16).astype(F32)
                tail = jnp.where(low_lanes, tail - tail_high, tail_high).astype(BF16)
                columns.append(dot(jnp.concatenate([high, low, high, tail], axis=1), zi[...]))
            high, low = halves(jnp.concatenate(columns, axis=1))
            cells = dot(ti[...], jnp.concatenate([high, low, high], axis=0))
            for field in range(2):
                mine = cells[:, NZ * field : NZ * (field + 1)]
                inner = mine[:OWN].reshape(SPAN, BY, NZ)
                edge = mine[OWN:].reshape(6, 24, NZ)
                if box == 0:
                    out[field, 1:19] = inner
                    out_pk[:, field, 0:24] = edge
                else:
                    out[field, 17:19] += inner[:2]
                    out[field, 19:35] = inner[2:]
                    out_pk[:, field, 16:24] += edge[:, :8]
                    out_pk[:, field, 24:40] = edge[:, 8:]

    for (present, copy), number in zip(first, origin):

        @pl.when(sides[number][1])
        def _():
            copy.wait_recv()

    for side in range(2):
        for field in range(2):
            r_pk[side, field, 2:34] = r_recv[side, field]
    for corner, (side, spot) in enumerate(((0, 1), (1, 34), (1, 1), (0, 34))):
        for field in range(2):
            r_pk[side, field, spot : spot + 1] = r_corner[corner, field : field + 1]
    apply_boxes(r_own, r_pk, u1, p1)
    finish_send(first)

    def exchange(width, own, packed, x_layers, x_corner, x_corner_send, y_rows, corners, corners_send, slot):
        low_layer = 1
        high_layer = 35 - width
        rows_low = packed.at[0:width]
        rows_high = packed.at[6 - width : 6]
        for side in range(2):
            for place, row in enumerate((0, 5)):
                x_corner_send[side, place] = packed[row, :, 32 * side : 32 * side + 4]
        for corner, (x_side, y_side) in enumerate(((0, 0), (1, 1), (0, 1), (1, 0))):
            start_row = (6 - width) * y_side
            for place in range(width):
                corners_send[corner, place] = packed[start_row + place, :, 32 * x_side : 32 * x_side + 4]
        return [
            remote(0, own.at[:, low_layer : low_layer + width], x_layers.at[1], slot),
            remote(1, own.at[:, high_layer : high_layer + width], x_layers.at[0], slot + 1),
            remote(2, rows_low, y_rows.at[1], slot + 2),
            remote(3, rows_high, y_rows.at[0], slot + 3),
            remote(4, corners_send.at[0], corners.at[1], slot + 4),
            remote(5, corners_send.at[1], corners.at[0], slot + 5),
            remote(6, corners_send.at[2], corners.at[3], slot + 6),
            remote(7, corners_send.at[3], corners.at[2], slot + 7),
            remote(0, x_corner_send.at[0], x_corner.at[1], slot + 8),
            remote(1, x_corner_send.at[1], x_corner.at[0], slot + 9),
        ]

    origin10 = origin + [1, 0]
    second = exchange(3, u1, p1, xl1, xc1, xcs1, yr1, dg1, dgs1, 12)
    start(second)

    for (present, copy), number in zip(zone_x, origin[:2]):

        @pl.when(sides[number][1])
        def _():
            copy.wait_recv()

    finish_send(zone_x)
    for side, name in enumerate(("xm", "xp")):

        @pl.when(jnp.logical_not(has[name]))
        def _():
            edge = zone[2 + 31 * side]
            zone[34 * side] = edge
            zone[34 * side + 1] = edge

    for place, row in enumerate((0, 1, 14, 15)):
        zone_send[place] = jnp.zeros((PX, NZ), jnp.int32)
        zone_send[place, 0:LX] = zone[:, row]
    zone_y = [
        remote(2, zone_send.at[0:2], zone_recv.at[1], 10),
        remote(3, zone_send.at[2:4], zone_recv.at[0], 11),
    ]
    start(zone_y)
    for layer in (0, 1, 34, 35):
        k0, k1, c0, c1, share = lookup(zone[layer], table)
        k_own[layer, 8:24] = k0
        k_own[LX + layer, 8:24] = k1
        c_own[0, layer] = c0
        c_own[1, layer] = c1
        cross[layer] = share * jnp.sqrt(c0 * c1)
    for (present, copy), number in zip(zone_y, origin[2:4]):

        @pl.when(sides[number][1])
        def _():
            copy.wait_recv()

    finish_send(zone_y)
    for side, name in enumerate(("ym", "yp")):

        @pl.when(jnp.logical_not(has[name]))
        def _():
            edge = zone_send[3 * side]
            zone_recv[side, 0] = edge
            zone_recv[side, 1] = edge

    for place in range(6):
        packed_zone = (
            zone_recv[0, place] if place < 2
            else zone_send[0] if place == 2
            else zone_send[3] if place == 3
            else zone_recv[1, place - 4]
        )
        k0, k1, c0, c1, share = lookup(packed_zone, table)
        k_pk[place, 0] = k0
        k_pk[place, 1] = k1
        if place in (1, 4):
            side = 0 if place == 1 else 1
            c_pk[side, 0] = c0
            c_pk[side, 1] = c1
            cross_pk[side] = share * jnp.sqrt(c0 * c1)
            for field, value in enumerate((k0, k1)):
                k_own[LX * field : LX * (field + 1), 7 if side == 0 else 24] = value[:LX]

    lanes = lax.broadcasted_iota(jnp.int32, (BY, NZ), 1)
    first_lane, last_lane = lanes == 0, lanes == NZ - 1
    for field in range(2):
        fx[field, 0] = 0.5 * (k_own[LX * field, 8:24] + k_own[LX * field + 1, 8:24])

    def faces(layer, carry):
        for field in range(2):
            spot = LX * field + layer
            center = k_own[spot, 8:24]
            x_low = fx[field, layer - 1]
            x_high = 0.5 * (center + k_own[spot + 1, 8:24])
            fx[field, layer] = x_high
            y_low = 0.5 * (center + k_own[spot, 7:23])
            y_high = 0.5 * (center + k_own[spot, 9:25])
            z_low = 0.5 * (center + jnp.where(first_lane, center, pltpu.roll(center, 1, axis=1)))
            z_high = 0.5 * (center + jnp.where(last_lane, center, pltpu.roll(center, NZ - 1, axis=1)))
            fym[field, layer] = y_low
            fyp[field, layer] = y_high
            fzm[field, layer] = jnp.where(first_lane, 0.0, z_low)
            fzp[field, layer] = jnp.where(last_lane, 0.0, z_high)
            diag[field, layer] = c_own[field, layer] + (
                (x_low + x_high) + (y_low + y_high) + (z_low + z_high)
            )
        return carry

    lax.fori_loop(1, 35, faces, 0)

    lanes_pk = lax.broadcasted_iota(jnp.int32, (PX, NZ), 1)
    first_pk, last_pk = lanes_pk == 0, lanes_pk == NZ - 1
    rows_pk = lax.broadcasted_iota(jnp.int32, (PX, NZ), 0)

    def rim_faces(side, field):
        center = k_pk[1 + 3 * side, field]
        x_low = 0.5 * (center + pltpu.roll(center, 1, axis=0))
        x_high = 0.5 * (center + pltpu.roll(center, PX - 1, axis=0))
        y_low = 0.5 * (center + k_pk[3 * side, field])
        y_high = 0.5 * (center + k_pk[3 * side + 2, field])
        z_low = 0.5 * (center + jnp.where(first_pk, center, pltpu.roll(center, 1, axis=1)))
        z_high = 0.5 * (center + jnp.where(last_pk, center, pltpu.roll(center, NZ - 1, axis=1)))
        return x_low, x_high, y_low, y_high, z_low, z_high

    def outside(value, present):
        return jnp.where(present, value, 0.0)

    for (present, copy), number in zip(second, origin10):

        @pl.when(sides[number][1])
        def _():
            copy.wait_recv()

    def assemble(width, own, packed, x_layers, x_corner, y_rows, corners, total_v, total_pk, margin):
        low0, high0 = 3 - width, 33
        for field in range(2):
            base = LX * field

            def copy_layer(layer, carry):
                total_v[base + layer, 8:24] = own[field, layer]
                return carry

            lax.fori_loop(3, 33, copy_layer, 0)
            for step in range(width):
                layer = low0 + step
                value = x_layers[0, field, step]
                if layer >= 1:
                    value = value + own[field, layer]
                if layer < 2:
                    value = outside(value, has["xm"])
                total_v[base + layer, 8:24] = value
                layer = high0 + step
                value = x_layers[1, field, step]
                if layer <= 34:
                    value = value + own[field, layer]
                if layer > 33:
                    value = outside(value, has["xp"])
                total_v[base + layer, 8:24] = value
        for side in range(2):
            for step in range(width):
                y = 1 - width + step if side == 0 else 15 + step
                place = y + 2 if side == 0 else y - 12
                total_pk[place] = y_rows[side, step]
                minus, plus = (0, 3) if side == 0 else (2, 1)
                total_pk[place, :, 0:4] += corners[minus, step]
                total_pk[place, :, 32:36] += corners[plus, step]
                if y == -1 or y == 16:
                    total_pk[place] += packed[5 * side]
                    total_pk[place, :, 0:4] += x_corner[0, side]
                    total_pk[place, :, 32:36] += x_corner[1, side]
                if y < 0 or y > 15:
                    present = has["ym"] if side == 0 else has["yp"]
                    low_x = jnp.logical_and(rows_pk < 2, jnp.logical_not(has["xm"]))
                    high_x = jnp.logical_and(rows_pk > 33, jnp.logical_not(has["xp"]))
                    drop = jnp.logical_or(jnp.logical_or(low_x, high_x), jnp.logical_not(present))
                    for field in range(2):
                        total_pk[place, field] = jnp.where(drop, 0.0, total_pk[place, field])
        for field in range(2):
            lo = 2 - margin
            count = BX + 2 * margin
            for side, row, halo in ((0, 8, 7), (1, 23, 24)):
                place = 2 if side == 0 else 3
                window = slice(LX * field + lo, LX * field + lo + count)
                added = total_pk[place, field, lo : lo + count]
                spots = lax.broadcasted_iota(jnp.int32, (count, NZ), 0) + lo
                low_x = jnp.logical_and(spots < 2, jnp.logical_not(has["xm"]))
                high_x = jnp.logical_and(spots > 33, jnp.logical_not(has["xp"]))
                added = jnp.where(jnp.logical_or(low_x, high_x), 0.0, added)
                edge = total_v[window, row] + added
                total_v[window, row] = edge
                if margin > 1:
                    total_pk[place, field, lo : lo + count] = edge
                outer = 1 if side == 0 else 4
                total_v[window, halo] = total_pk[outer, field, lo : lo + count]

    assemble(3, u1, p1, xl1, xc1, yr1, dg1, v1, zp, 2)

    def operate(vec, layer, field):
        spot = LX * field + layer
        center = vec[spot, 8:24]
        value = diag[field, layer] * center + cross[layer] * vec[LX * (1 - field) + layer, 8:24]
        value = value - fx[field, layer - 1] * vec[spot - 1, 8:24] - fx[field, layer] * vec[spot + 1, 8:24]
        value = value - fym[field, layer] * vec[spot, 7:23] - fyp[field, layer] * vec[spot, 9:25]
        value = value - fzm[field, layer] * pltpu.roll(center, 1, axis=1)
        return value - fzp[field, layer] * pltpu.roll(center, NZ - 1, axis=1), center

    def fold(value):
        return value[:8] + value[8:]

    def first_image(layer, carry):
        rz, pq = carry
        for field in range(2):
            value, center = operate(v1, layer, field)
            q_own[field, layer] = value
            rz = rz + fold(r_own[field, layer] * center)
            pq = pq + fold(center * value)
        return rz, pq

    rz, pq = lax.fori_loop(2, 34, first_image, (zero, zero))
    for layer, name in ((1, "xm"), (34, "xp")):
        for field in range(2):
            value, _ = operate(v1, layer, field)
            q_own[field, layer] = outside(value, has[name])
    for side, name in enumerate(("ym", "yp")):
        center_place = 1 + 3 * side
        for field in range(2):
            x_low, x_high, y_low, y_high, z_low, z_high = rim_faces(side, field)
            center = zp[center_place, field]
            value = c_pk[side, field] + ((x_low + x_high) + (y_low + y_high) + (z_low + z_high))
            value = value * center + cross_pk[side] * zp[center_place, 1 - field]
            value = value - x_low * pltpu.roll(center, 1, axis=0) - x_high * pltpu.roll(center, PX - 1, axis=0)
            value = value - y_low * zp[3 * side, field] - y_high * zp[3 * side + 2, field]
            value = value - jnp.where(first_pk, 0.0, z_low) * pltpu.roll(center, 1, axis=1)
            value = value - jnp.where(last_pk, 0.0, z_high) * pltpu.roll(center, NZ - 1, axis=1)
            low_x = jnp.logical_and(rows_pk < 2, jnp.logical_not(has["xm"]))
            high_x = jnp.logical_and(rows_pk > 33, jnp.logical_not(has["xp"]))
            drop = jnp.logical_or(jnp.logical_or(low_x, high_x), jnp.logical_not(has[name]))
            unused_rows = jnp.logical_or(rows_pk < 1, rows_pk > 34)
            q_pk[side, field] = jnp.where(jnp.logical_or(drop, unused_rows), 0.0, value)

    apply_boxes(q_own, q_pk, u2, p2)
    third = exchange(2, u2, p2, xl2, xc2, xcs2, yr2, dg2, dgs2, 22)
    start(third)
    finish_send(second)
    for (present, copy), number in zip(third, origin10):

        @pl.when(sides[number][1])
        def _():
            copy.wait_recv()

    assemble(2, u2, p2, xl2, xc2, yr2, dg2, v2, wp, 1)

    def second_image(layer, carry):
        rw, qw, zu, wu = carry
        for field in range(2):
            value, center = operate(v2, layer, field)
            u_vec[field, layer] = value
            rw = rw + fold(r_own[field, layer] * center)
            qw = qw + fold(q_own[field, layer] * center)
            zu = zu + fold(v1[LX * field + layer, 8:24] * value)
            wu = wu + fold(center * value)
        return rw, qw, zu, wu

    rw, qw, zu, wu = lax.fori_loop(2, 34, second_image, (zero,) * 4)
    finish_send(third)

    sums = [jnp.sum(v, axis=0, keepdims=True) for v in (rz, pq, rw, qw, zu, wu)]
    ar1[0] = jnp.concatenate(sums + [jnp.zeros((2, NZ), F32)], axis=0)

    def all_reduce(slots, count, device_of, number):
        def send(k, carry):
            pltpu.make_async_remote_copy(
                src_ref=slots.at[0],
                dst_ref=slots.at[k],
                send_sem=ar_send.at[number],
                recv_sem=ar_recv.at[number],
                device_id=device_of(k),
                device_id_type=MESH,
            ).start()
            return carry

        lax.fori_loop(1, count, send, 0)
        others = slots.at[1:count]
        pltpu.make_async_copy(others, others, ar_recv.at[number]).wait()
        pltpu.make_async_copy(others, others, ar_send.at[number]).wait()
        return jnp.sum(slots[...], axis=0)

    ar2[0] = all_reduce(ar1, plane, plane_id, 0)
    products = jnp.sum(all_reduce(ar2, depth, depth_id, 1), axis=1, keepdims=True)
    rz, pq, rw, qw, zu, wu = (products[n : n + 1] for n in range(6))
    alpha = rz / pq
    rz2 = rz - alpha * (rw + pq) + alpha * alpha * qw
    grow = 1.0 + rz2 / rz
    curve = grow * grow * pq - grow * alpha * (zu + qw) + alpha * alpha * wu
    alpha2 = rz2 / curve
    by_z = jnp.broadcast_to(alpha + alpha2 * grow, (BY, NZ))
    by_w = jnp.broadcast_to(alpha2 * alpha, (BY, NZ))

    def finish(layer, carry):
        for field in range(2):
            spot = LX * field + layer
            x_out[field, layer - 2] = by_z * v1[spot, 8:24] - by_w * v2[spot, 8:24]
            r_out[field, layer - 2] = (
                r_own[field, layer] - by_z * q_own[field, layer] + by_w * u_vec[field, layer]
            )
        return carry

    lax.fori_loop(2, 34, finish, 0)


def shards(nx, ny, load, zones, conductance, capacity, coupling):
    to_modes, from_modes, z_forward, z_inverse, summed, group = constants()
    ax, ay = min(8, nx // 2), min(4, ny // 2)
    plane, depth = ax * ay, (nx // ax) * (ny // ay)
    vmem = lambda *shape, dtype=F32: pltpu.VMEM(shape, dtype)
    scratch = [
        vmem(*to_modes.shape, dtype=BF16), vmem(*from_modes.shape, dtype=BF16),
        vmem(*z_forward.shape, dtype=BF16), vmem(*z_inverse.shape, dtype=BF16),
        vmem(*summed.shape), vmem(*group.shape, dtype=BF16),
        vmem(2, LX, BY, NZ), vmem(2, 2, PX, NZ),
        vmem(LX, BY, NZ, dtype=jnp.int32), vmem(8, NZ, dtype=jnp.int32),
        vmem(4, PX, NZ, dtype=jnp.int32), vmem(2, 2, PX, NZ, dtype=jnp.int32),
        vmem(2, 2, BX, NZ), vmem(2, 2, BX, NZ), vmem(4, 2, NZ), vmem(4, 2, NZ),
        vmem(2 * LX, 32, NZ), vmem(6, 2, PX, NZ), vmem(2, LX, BY, NZ), vmem(2, 2, PX, NZ),
        vmem(LX, BY, NZ), vmem(2, PX, NZ),
        vmem(2, LX, BY, NZ), vmem(2, LX, BY, NZ), vmem(2, LX, BY, NZ), vmem(2, LX, BY, NZ),
        vmem(2, LX, BY, NZ), vmem(2, LX, BY, NZ), vmem(8, NZ), vmem(4, MODES, 256),
        vmem(2, LX, BY, NZ), vmem(6, 2, PX, NZ), vmem(2 * LX, 32, NZ), vmem(6, 2, PX, NZ),
        vmem(2, LX, BY, NZ), vmem(2, 2, PX, NZ),
        vmem(2, LX, BY, NZ), vmem(6, 2, PX, NZ), vmem(2 * LX, 32, NZ), vmem(6, 2, PX, NZ),
        vmem(2, LX, BY, NZ),
    ]
    for width in (3, 2):
        scratch += [
            vmem(2, 2, width, BY, NZ), vmem(2, 2, 2, 4, NZ), vmem(2, 2, 2, 4, NZ),
            vmem(2, width, 2, PX, NZ), vmem(4, width, 2, 4, NZ), vmem(4, width, 2, 4, NZ),
        ]
    scratch += [
        vmem(plane, 8, NZ), vmem(depth, 8, NZ),
        pltpu.SemaphoreType.DMA((9,)), pltpu.SemaphoreType.DMA((32,)), pltpu.SemaphoreType.DMA((32,)),
        pltpu.SemaphoreType.DMA((2,)), pltpu.SemaphoreType.DMA((2,)),
    ]
    any_spec = pl.BlockSpec(memory_space=pl.ANY)
    smem = pl.BlockSpec(memory_space=pltpu.SMEM)
    out = pl.BlockSpec(memory_space=pltpu.VMEM)
    shape = jax.ShapeDtypeStruct((2, BX, BY, NZ), F32)
    return pl.pallas_call(
        functools.partial(body, nx, ny),
        out_shape=(shape, shape),
        in_specs=[any_spec, any_spec, smem, smem, smem] + [any_spec] * 6,
        out_specs=(out, out),
        scratch_shapes=scratch,
        compiler_params=pltpu.CompilerParams(
            collective_id=0, has_side_effects=True, vmem_limit_bytes=48 * 1024 * 1024
        ),
        name="pcg",
    )(
        load, zones, conductance, capacity, coupling,
        *(jnp.asarray(c) for c in (to_modes, from_modes, z_forward, z_inverse, summed, group)),
    )


def solution(mesh):
    in_specs = (P(None, "gx", "gy", None), P("gx", "gy", None), P(), P(), P())
    out_specs = (P(None, "gx", "gy", None), P(None, "gx", "gy", None))
    run = functools.partial(shards, mesh.shape["gx"], mesh.shape["gy"])
    return jax.shard_map(run, mesh=mesh, in_specs=in_specs, out_specs=out_specs, check_vma=False)
```

time: 609 us -> 85.8 us (0.14)
  blocking collectives: 406 us -> 0 us
  Pallas kernels: 0 us -> 73.2 us
  starting transfers between devices: 70.7 us -> 0 us
  other arithmetic: 46.1 us -> 0 us
  waiting for transfers between devices: 36 us -> 0 us
  matrix products: 25.9 us -> 0 us
    psum x3 -> x0, blocking collectives: 406 us -> none  [the longest x2 285 us: shards(): product = lax.psum(jnp.sum(residual * precond), ('gx', 'gy'))]
    pallas_call x0 -> x1, Pallas kernels: none -> 73.2 us  [shards(): pl.pallas_call(functools.partial(body, nx, ny), out_shape=(shape, shape),...]
    ppermute x28 -> x0, starting transfers between devices: 70.7 us -> none  [the longest x14 39.1 us: with_halo(): lax.ppermute(lax.slice_in_dim(block, block.shape[dim] - width, None, axis...]
    ppermute x28 -> x0, waiting for transfers between devices: 36 us -> none  [the longest x14 35.9 us: with_halo(): lax.ppermute(lax.slice_in_dim(block, 0, width, axis=dim), axis, backward)]
    add x9 -> x0, other arithmetic: 29.6 us -> none  [the longest x2 19.7 us: apply_operator(): flux + face * (field - neighbour(padded, offset_x, offset_y, offset_z))]
    dot_general x13 -> x0, matrix products: 25.9 us -> none  [the longest x2 4.65 us: solve_boxes(): jnp.einsum('co,fabc->fabo', matrix_z, spectral, precision=highest)]
    concatenate x6 -> x0, other arithmetic: 7.12 us -> none  [with_halo(): block = jnp.concatenate([low, block, high], axis=dim)]
  transfers between devices with their start and end apart: 28 -> 0, of which waited for: 10 -> 0; matrix products, arithmetic and copies ran while one was open for 2% -> 0% of each run, Pallas kernels for 0% -> 0%
where the time goes in v1:
time: 85.8 us; the launch traced here: 85.4 us
  Pallas kernels  73.2 us (85%)
  local copies, waits for them, and re-layouts  11.6 us (14%)
    pallas_call x1, Pallas kernels, shards(): pl.pallas_call(functools.partial(body, nx, ny), out_shape=(shape, shape),...  73.2 us
    unnamed x24, local copies, waits for them, and re-layouts  11.6 us

profile of v1, /device:TPU:1, one launch (start us, length us, event | category | flops | bytes accessed | tf_op | source)
XLA Modules:
  0.0 85.4 jit_solution(6729767929105342955)
XLA Ops:
  0.6 0.0 copy-start
  0.6 1.2 %copy-done = bf16[432,1008]{1,0:T(8,128)(2,1)S(1)} copy-done((bf16[432,1008]{1,0:T(8,128)(2,1)S(1)}, bf16[432,1008]{1,0:T(8,128)(2,1)}, u32[]{:S(2)}) %copy-start) | copy-done | bytes 870936
  1.8 0.0 copy-start.1
  1.8 1.1 %copy-done.1 = bf16[336,1008]{1,0:T(8,128)(2,1)S(1)} copy-done((bf16[336,1008]{1,0:T(8,128)(2,1)S(1)}, bf16[336,1008]{1,0:T(8,128)(2,1)}, u32[]{:S(2)}) %copy-start.1) | copy-done | bytes 677400
  2.9 0.0 copy-start.2
  2.9 1.0 %copy-done.2 = f32[2,32,16,128]{3,2,1,0:T(8,128)S(1)} copy-done((f32[2,32,16,128]{3,2,1,0:T(8,128)S(1)}, f32[2,32,16,128]{3,2,1,0:T(8,128)}, u32[]{:S(2)}) %copy-start.2) | copy-done | bytes 524312
  3.9 0.0 copy-start.3
  3.9 1.0 %copy-done.3 = f32[336,256]{1,0:T(8,128)S(1)} copy-done((f32[336,256]{1,0:T(8,128)S(1)}, f32[336,256]{1,0:T(8,128)}, u32[]{:S(2)}) %copy-start.3) | copy-done | bytes 344088
  4.9 0.0 copy-start.4
  4.9 0.9 %copy-done.4 = s32[32,16,128]{2,1,0:T(8,128)S(1)} copy-done((s32[32,16,128]{2,1,0:T(8,128)S(1)}, s32[32,16,128]{2,1,0:T(8,128)}, u32[]{:S(2)}) %copy-start.4) | copy-done | bytes 262168
  5.9 0.0 copy-start.5
  5.9 0.9 %copy-done.5 = bf16[384,256]{1,0:T(8,128)(2,1)S(1)} copy-done((bf16[384,256]{1,0:T(8,128)(2,1)S(1)}, bf16[384,256]{1,0:T(8,128)(2,1)}, u32[]{:S(2)}) %copy-start.5) | copy-done | bytes 196632
  6.8 0.0 copy-start.6
  6.8 0.9 %copy-done.6 = bf16[384,256]{1,0:T(8,128)(2,1)S(1)} copy-done((bf16[384,256]{1,0:T(8,128)(2,1)S(1)}, bf16[384,256]{1,0:T(8,128)(2,1)}, u32[]{:S(2)}) %copy-start.6) | copy-done | bytes 196632
  7.7 0.0 copy-start.7
  7.7 0.9 %copy-done.7 = bf16[512,128]{1,0:T(8,128)(2,1)S(1)} copy-done((bf16[512,128]{1,0:T(8,128)(2,1)S(1)}, bf16[512,128]{1,0:T(8,128)(2,1)}, u32[]{:S(2)}) %copy-start.7) | copy-done | bytes 131096
  8.6 0.0 copy-start.8
  8.6 0.7 copy-done.8
  9.3 0.0 copy-start.9
  9.3 0.7 copy-done.9
  10.0 0.0 copy-start.10
  10.0 0.7 copy-done.10
  10.6 73.2 %pcg.1 = (f32[2,32,16,128]{3,2,1,0:T(8,128)S(1)}, f32[2,32,16,128]{3,2,1,0:T(8,128)S(1)}) custom-call(f32[2,32,16,128]{3,2,1,0:T(8,128)S(1)} %copy-done.2, s32[32,16,128]{2,1,0:T(8,128)S(1)} %copy-done.4, f32[2,8]{1,0:T(2,128)S(1)} %copy-done.8, f32[2,8]{1,0:T(2,128)S(1)} %copy-done.9, f32[8]{0:T(128)S(1)} %copy-done.10, bf16[336,1008]{1,0:T(8,128)(2,1)S(1)} %copy-done.1, ...), custom_call_target="tpu_custom_call" | custom-call | tf_op jit(solution)/shard_map/pcg/pallas_call | solution.py:714
  83.8 0.8 copy.15
  84.6 0.8 copy.16
Async XLA Ops:
  0.6 1.2 %copy-start = (bf16[432,1008]{1,0:T(8,128)(2,1)S(1)}, bf16[432,1008]{1,0:T(8,128)(2,1)}, u32[]{:S(2)}) copy-start(bf16[432,1008]{1,0:T(8,128)(2,1)} %constant.13.clone.ti_hbm) | copy-start | bytes 2612740
  1.8 1.1 %copy-start.1 = (bf16[336,1008]{1,0:T(8,128)(2,1)S(1)}, bf16[336,1008]{1,0:T(8,128)(2,1)}, u32[]{:S(2)}) copy-start(bf16[336,1008]{1,0:T(8,128)(2,1)} %constant.12.clone.tf_hbm) | copy-start | bytes 2032132
  2.9 1.0 %copy-start.2 = (f32[2,32,16,128]{3,2,1,0:T(8,128)S(1)}, f32[2,32,16,128]{3,2,1,0:T(8,128)}, u32[]{:S(2)}) copy-start(f32[2,32,16,128]{3,2,1,0:T(8,128)} %load_ref.1) | copy-start | bytes 1572868
  3.9 1.0 %copy-start.3 = (f32[336,256]{1,0:T(8,128)S(1)}, f32[336,256]{1,0:T(8,128)}, u32[]{:S(2)}) copy-start(f32[336,256]{1,0:T(8,128)} %constant.16.clone.lam_hbm) | copy-start | bytes 1032196
  4.9 0.9 %copy-start.4 = (s32[32,16,128]{2,1,0:T(8,128)S(1)}, s32[32,16,128]{2,1,0:T(8,128)}, u32[]{:S(2)}) copy-start(s32[32,16,128]{2,1,0:T(8,128)} %zones_ref.1) | copy-start | bytes 786436
  5.9 0.9 %copy-start.5 = (bf16[384,256]{1,0:T(8,128)(2,1)S(1)}, bf16[384,256]{1,0:T(8,128)(2,1)}, u32[]{:S(2)}) copy-start(bf16[384,256]{1,0:T(8,128)(2,1)} %constant.17.clone.group_hbm) | copy-start | bytes 589828
  6.8 0.9 %copy-start.6 = (bf16[384,256]{1,0:T(8,128)(2,1)S(1)}, bf16[384,256]{1,0:T(8,128)(2,1)}, u32[]{:S(2)}) copy-start(bf16[384,256]{1,0:T(8,128)(2,1)} %constant.14.clone.zf_hbm) | copy-start | bytes 589828
  7.7 0.9 %copy-start.7 = (bf16[512,128]{1,0:T(8,128)(2,1)S(1)}, bf16[512,128]{1,0:T(8,128)(2,1)}, u32[]{:S(2)}) copy-start(bf16[512,128]{1,0:T(8,128)(2,1)} %constant.15.clone.zi_hbm) | copy-start | bytes 393220
  8.6 0.7 copy-start.8
  9.3 0.7 copy-start.9
  10.0 0.7 copy-start.10

commit v2 on v1

--- a/solution.py
+++ b/solution.py
@@ -110,10 +110,10 @@
 
 def body(
     nx, ny,
-    load_ref, zones_ref, cond_ref, cap_ref, coup_ref,
+    load_ref, zones_ref, cond_hbm, cap_hbm, coup_hbm,
     tf_hbm, ti_hbm, zf_hbm, zi_hbm, lam_hbm, group_hbm,
     x_out, r_out,
-    tf, ti, zf, zi, lam, group,
+    cond_ref, cap_ref, coup_ref, tf, ti, zf, zi, lam, group,
     r_own, r_pk, zone, zone_pk, zone_send, zone_recv,
     r_send, r_recv, r_corner_send, r_corner,
     k_own, k_pk, c_own, c_pk, cross, cross_pk,
@@ -128,16 +128,20 @@
     has = {"xm": gx > 0, "xp": gx < nx - 1, "ym": gy > 0, "yp": gy < ny - 1}
     ax, ay = min(8, nx // 2), min(4, ny // 2)
     plane, depth = ax * ay, (nx // ax) * (ny // ay)
-    here = (gx % ax) * ay + gy % ay
-    level = (gx // ax) * (ny // ay) + gy // ay
+    div, rem = lax.div, lax.rem
+    across, along = nx // ax, ny // ay
+    gx_block, gx_in = div(gx, jnp.int32(ax)), rem(gx, jnp.int32(ax))
+    gy_block, gy_in = div(gy, jnp.int32(ay)), rem(gy, jnp.int32(ay))
+    here = gx_in * ay + gy_in
+    level = gx_block * along + gy_block
 
     def plane_id(k):
-        t = (here + k) % plane
-        return ((gx // ax) * ax + t // ay, (gy // ay) * ay + t % ay)
+        t = rem(here + k, jnp.int32(plane))
+        return (gx_block * ax + div(t, jnp.int32(ay)), gy_block * ay + rem(t, jnp.int32(ay)))
 
     def depth_id(k):
-        t = (level + k) % depth
-        return ((t // (ny // ay)) * ax + gx % ax, (t % (ny // ay)) * ay + gy % ay)
+        t = rem(level + k, jnp.int32(depth))
+        return (div(t, jnp.int32(along)) * ax + gx_in, rem(t, jnp.int32(along)) * ay + gy_in)
 
     sides = [
         ("xm", has["xm"], (gx - 1, gy)),
@@ -154,6 +158,9 @@
         pltpu.make_async_copy(load_ref.at[0], r_own.at[0, 2:34], local_sem.at[0]),
         pltpu.make_async_copy(load_ref.at[1], r_own.at[1, 2:34], local_sem.at[1]),
         pltpu.make_async_copy(zones_ref, zone.at[2:34], local_sem.at[2]),
+        pltpu.make_async_copy(cond_hbm, cond_ref, local_sem.at[9]),
+        pltpu.make_async_copy(cap_hbm, cap_ref, local_sem.at[10]),
+        pltpu.make_async_copy(coup_hbm, coup_ref, local_sem.at[11]),
     ]
     weights = [
         pltpu.make_async_copy(source, target, local_sem.at[3 + n])
@@ -382,8 +389,16 @@
         ]
 
     origin10 = origin + [1, 0]
+
+    def start_far_first(copies):
+        along_y = copies[2:4]
+        others = copies[:2] + copies[8:] + copies[4:8]
+        start(others)
+        finish_send(others)
+        start(along_y)
+
     second = exchange(3, u1, p1, xl1, xc1, xcs1, yr1, dg1, dgs1, 12)
-    start(second)
+    start_far_first(second)
 
     for (present, copy), number in zip(zone_x, origin[:2]):
 
@@ -473,7 +488,7 @@
             )
         return carry
 
-    lax.fori_loop(1, 35, faces, 0)
+    lax.fori_loop(1, 35, faces, 0, unroll=2)
 
     lanes_pk = lax.broadcasted_iota(jnp.int32, (PX, NZ), 1)
     first_pk, last_pk = lanes_pk == 0, lanes_pk == NZ - 1
@@ -507,7 +522,7 @@
                 total_v[base + layer, 8:24] = own[field, layer]
                 return carry
 
-            lax.fori_loop(3, 33, copy_layer, 0)
+            lax.fori_loop(3, 33, copy_layer, 0, unroll=6)
             for step in range(width):
                 layer = low0 + step
                 value = x_layers[0, field, step]
@@ -583,7 +598,7 @@
             pq = pq + fold(center * value)
         return rz, pq
 
-    rz, pq = lax.fori_loop(2, 34, first_image, (zero, zero))
+    rz, pq = lax.fori_loop(2, 34, first_image, (zero, zero), unroll=4)
     for layer, name in ((1, "xm"), (34, "xp")):
         for field in range(2):
             value, _ = operate(v1, layer, field)
@@ -607,8 +622,8 @@
 
     apply_boxes(q_own, q_pk, u2, p2)
     third = exchange(2, u2, p2, xl2, xc2, xcs2, yr2, dg2, dgs2, 22)
-    start(third)
-    finish_send(second)
+    start_far_first(third)
+    finish_send(second[2:4])
     for (present, copy), number in zip(third, origin10):
 
         @pl.when(sides[number][1])
@@ -628,11 +643,14 @@
             wu = wu + fold(center * value)
         return rw, qw, zu, wu
 
-    rw, qw, zu, wu = lax.fori_loop(2, 34, second_image, (zero,) * 4)
-    finish_send(third)
-
-    sums = [jnp.sum(v, axis=0, keepdims=True) for v in (rz, pq, rw, qw, zu, wu)]
-    ar1[0] = jnp.concatenate(sums + [jnp.zeros((2, NZ), F32)], axis=0)
+    rw, qw, zu, wu = lax.fori_loop(2, 34, second_image, (zero,) * 4, unroll=4)
+    finish_send(third[2:4])
+
+    spot = lax.broadcasted_iota(jnp.int32, (1, NZ), 1)
+    row = jnp.zeros((1, NZ), F32)
+    for place, value in enumerate((rz, pq, rw, qw, zu, wu)):
+        row = jnp.where(spot == place, jnp.sum(value), row)
+    ar1[0] = row
 
     def all_reduce(slots, count, device_of, number):
         def send(k, carry):
@@ -646,15 +664,18 @@
             ).start()
             return carry
 
-        lax.fori_loop(1, count, send, 0)
+        for k in range(1, count):
+            send(k, 0)
         others = slots.at[1:count]
         pltpu.make_async_copy(others, others, ar_recv.at[number]).wait()
         pltpu.make_async_copy(others, others, ar_send.at[number]).wait()
         return jnp.sum(slots[...], axis=0)
 
     ar2[0] = all_reduce(ar1, plane, plane_id, 0)
-    products = jnp.sum(all_reduce(ar2, depth, depth_id, 1), axis=1, keepdims=True)
-    rz, pq, rw, qw, zu, wu = (products[n : n + 1] for n in range(6))
+    products = all_reduce(ar2, depth, depth_id, 1)
+    rz, pq, rw, qw, zu, wu = (
+        jnp.sum(jnp.where(spot == n, products, 0.0), axis=1, keepdims=True) for n in range(6)
+    )
     alpha = rz / pq
     rz2 = rz - alpha * (rw + pq) + alpha * alpha * qw
     grow = 1.0 + rz2 / rz
@@ -672,7 +693,7 @@
             )
         return carry
 
-    lax.fori_loop(2, 34, finish, 0)
+    lax.fori_loop(2, 34, finish, 0, unroll=4)
 
 
 def shards(nx, ny, load, zones, conductance, capacity, coupling):
@@ -681,6 +702,7 @@
     plane, depth = ax * ay, (nx // ax) * (ny // ay)
     vmem = lambda *shape, dtype=F32: pltpu.VMEM(shape, dtype)
     scratch = [
+        pltpu.SMEM((2, ZONES), F32), pltpu.SMEM((2, ZONES), F32), pltpu.SMEM((ZONES,), F32),
         vmem(*to_modes.shape, dtype=BF16), vmem(*from_modes.shape, dtype=BF16),
         vmem(*z_forward.shape, dtype=BF16), vmem(*z_inverse.shape, dtype=BF16),
         vmem(*summed.shape), vmem(*group.shape, dtype=BF16),
@@ -703,18 +725,17 @@
             vmem(2, width, 2, PX, NZ), vmem(4, width, 2, 4, NZ), vmem(4, width, 2, 4, NZ),
         ]
     scratch += [
-        vmem(plane, 8, NZ), vmem(depth, 8, NZ),
-        pltpu.SemaphoreType.DMA((9,)), pltpu.SemaphoreType.DMA((32,)), pltpu.SemaphoreType.DMA((32,)),
+        vmem(plane, 1, NZ), vmem(depth, 1, NZ),
+        pltpu.SemaphoreType.DMA((12,)), pltpu.SemaphoreType.DMA((32,)), pltpu.SemaphoreType.DMA((32,)),
         pltpu.SemaphoreType.DMA((2,)), pltpu.SemaphoreType.DMA((2,)),
     ]
-    any_spec = pl.BlockSpec(memory_space=pl.ANY)
-    smem = pl.BlockSpec(memory_space=pltpu.SMEM)
+    any_spec = pl.BlockSpec(memory_space=pltpu.HBM)
     out = pl.BlockSpec(memory_space=pltpu.VMEM)
     shape = jax.ShapeDtypeStruct((2, BX, BY, NZ), F32)
     return pl.pallas_call(
         functools.partial(body, nx, ny),
         out_shape=(shape, shape),
-        in_specs=[any_spec, any_spec, smem, smem, smem] + [any_spec] * 6,
+        in_specs=[any_spec] * 11,
         out_specs=(out, out),
         scratch_shapes=scratch,
         compiler_params=pltpu.CompilerParams(
@@ -722,8 +743,8 @@
         ),
         name="pcg",
     )(
-        load, zones, conductance, capacity, coupling,
-        *(jnp.asarray(c) for c in (to_modes, from_modes, z_forward, z_inverse, summed, group)),
+        *(pltpu.with_memory_space_constraint(a, pltpu.HBM) for a in (load, zones, conductance, capacity, coupling)),
+        *(pltpu.with_memory_space_constraint(jnp.asarray(c), pltpu.HBM) for c in (to_modes, from_modes, z_forward, z_inverse, summed, group)),
     )
 
 

time: 85.8 us -> 67.8 us (0.79)
  local copies, waits for them, and re-layouts: 11.6 us -> 1.59 us
  Pallas kernels: 73.2 us -> 65.5 us
    unnamed x24 -> x2, local copies, waits for them, and re-layouts: 11.6 us -> 1.59 us
    pallas_call x1, Pallas kernels: 73.2 us -> 65.5 us  [shards(): pl.pallas_call(functools.partial(body, nx, ny), out_shape=(shape, shape),...]
where the time goes in v2:
time: 67.8 us; the launch traced here: 67.7 us
  Pallas kernels  65.5 us (97%)
  local copies, waits for them, and re-layouts  1.59 us (2%)
    pallas_call x1, Pallas kernels, shards(): pl.pallas_call(functools.partial(body, nx, ny), out_shape=(shape, shape),...  65.5 us
    unnamed x2, local copies, waits for them, and re-layouts  1.59 us

profile of v2, /device:TPU:1, one launch (start us, length us, event | category | flops | bytes accessed | tf_op | source)
XLA Modules:
  0.0 67.7 jit_solution(6694380215243239672)
XLA Ops:
  0.6 65.5 %pcg.1 = (f32[2,32,16,128]{3,2,1,0:T(8,128)S(1)}, f32[2,32,16,128]{3,2,1,0:T(8,128)S(1)}) custom-call(f32[2,32,16,128]{3,2,1,0:T(8,128)} %load_ref.1, s32[32,16,128]{2,1,0:T(8,128)} %zones_ref.1, f32[2,8]{1,0:T(2,128)} %cond_hbm.1, f32[2,8]{1,0:T(2,128)} %cap_hbm.1, f32[8]{0:T(128)} %coup_hbm.1, bf16[336,1008]{1,0:T(8,128)(2,1)} %constant.12.clone.tf_hbm, ...), custom_call_target="tpu_custom_call" | custom-call | tf_op jit(solution)/shard_map/pcg/pallas_call | solution.py:735
  66.1 0.8 %copy.15 = f32[2,32,16,128]{3,2,1,0:T(8,128)} copy(f32[2,32,16,128]{3,2,1,0:T(8,128)S(1)} %get-tuple-element.4) | data formatting | bytes 1048576
  66.9 0.8 %copy.16 = f32[2,32,16,128]{3,2,1,0:T(8,128)} copy(f32[2,32,16,128]{3,2,1,0:T(8,128)S(1)} %get-tuple-element.5) | data formatting | bytes 1048576

commit v3 on v2

--- a/solution.py
+++ b/solution.py
@@ -143,16 +143,16 @@
         t = rem(level + k, jnp.int32(depth))
         return (div(t, jnp.int32(along)) * ax + gx_in, rem(t, jnp.int32(along)) * ay + gy_in)
 
-    sides = [
-        ("xm", has["xm"], (gx - 1, gy)),
-        ("xp", has["xp"], (gx + 1, gy)),
-        ("ym", has["ym"], (gx, gy - 1)),
-        ("yp", has["yp"], (gx, gy + 1)),
-        ("mm", jnp.logical_and(has["xm"], has["ym"]), (gx - 1, gy - 1)),
-        ("pp", jnp.logical_and(has["xp"], has["yp"]), (gx + 1, gy + 1)),
-        ("mp", jnp.logical_and(has["xm"], has["yp"]), (gx - 1, gy + 1)),
-        ("pm", jnp.logical_and(has["xp"], has["ym"]), (gx + 1, gy - 1)),
-    ]
+    late = jnp.where(gx_in == 0, 0, 1).astype(jnp.int32)
+    near = 1 - late
+    near_gx, late_gx = gx + 1 - 2 * late, gx - 1 + 2 * late
+    near_here = jnp.logical_and(near_gx >= 0, near_gx < nx)
+    late_here = jnp.logical_and(late_gx >= 0, late_gx < nx)
+    y_here = (has["ym"], has["yp"])
+    sides = [(has["xm"], (gx - 1, gy)), (has["xp"], (gx + 1, gy)), (has["ym"], (gx, gy - 1)), (has["yp"], (gx, gy + 1))]
+    for c in range(4):
+        present = jnp.logical_and(sides[c // 2][0], y_here[c % 2])
+        sides.append((present, (gx - 1 + 2 * (c // 2), gy - 1 + 2 * (c % 2))))
 
     loads = [
         pltpu.make_async_copy(load_ref.at[0], r_own.at[0, 2:34], local_sem.at[0]),
@@ -172,7 +172,7 @@
         copy.start()
 
     barrier = pltpu.get_barrier_semaphore()
-    for _, present, device in sides:
+    for present, device in sides:
 
         @pl.when(present)
         def _():
@@ -193,7 +193,7 @@
         for ref in refs:
             ref[...] = jnp.zeros(ref.shape, ref.dtype)
 
-    r_pk[...] = jnp.zeros(r_pk.shape, F32)
+    clear(r_pk, u1, p1, u2, p2)
     for side, name in enumerate(("xm", "xp")):
 
         @pl.when(jnp.logical_not(has[name]))
@@ -209,7 +209,7 @@
 
     for corner in range(4):
 
-        @pl.when(jnp.logical_not(sides[4 + corner][1]))
+        @pl.when(jnp.logical_not(sides[4 + corner][0]))
         def _():
             clear(r_corner.at[corner], dg1.at[corner], dg2.at[corner])
 
@@ -219,64 +219,45 @@
     for field in range(2):
         r_send[0, field] = r_own[field, 2:34, 0]
         r_send[1, field] = r_own[field, 2:34, BY - 1]
-    for corner, (layer, row) in enumerate(((2, 0), (33, 15), (2, 15), (33, 0))):
+    for corner, (layer, row) in enumerate(((2, 0), (2, 15), (33, 0), (33, 15))):
         for field in range(2):
             r_corner_send[corner, field : field + 1] = r_own[field, layer, row : row + 1]
 
     members = jnp.int32(plane - 1 + depth - 1)
-    for _, present, _ in sides:
+    for present, _ in sides:
         members = members + present.astype(jnp.int32)
     pl.semaphore_wait(barrier, members)
 
-    def remote(number, source, target, slot):
-        _, present, device = sides[number]
-        return present, pltpu.make_async_remote_copy(
-            src_ref=source,
-            dst_ref=target,
-            send_sem=send_sem.at[slot],
-            recv_sem=recv_sem.at[slot],
-            device_id=device,
-            device_id_type=MESH,
-        )
-
-    def start(copies):
-        for present, copy in copies:
-
-            @pl.when(present)
-            def _():
-                copy.start()
-
-    def finish_recv(copies, arrives):
-        for (_, copy), number in zip(copies, arrives):
-
-            @pl.when(sides[number][1])
-            def _():
-                copy.wait_recv()
-
-    def finish_send(copies):
-        for present, copy in copies:
-
-            @pl.when(present)
-            def _():
-                copy.wait_send()
-
-    first = [
-        remote(0, r_own.at[:, 2], r_own.at[:, 34], 0),
-        remote(1, r_own.at[:, 33], r_own.at[:, 1], 1),
-        remote(2, r_send.at[0], r_recv.at[1], 2),
-        remote(3, r_send.at[1], r_recv.at[0], 3),
-        remote(4, r_corner_send.at[0], r_corner.at[1], 4),
-        remote(5, r_corner_send.at[1], r_corner.at[0], 5),
-        remote(6, r_corner_send.at[2], r_corner.at[3], 6),
-        remote(7, r_corner_send.at[3], r_corner.at[2], 7),
-    ]
-    origin = [1, 0, 3, 2, 5, 4, 7, 6]
-    start(first)
-    zone_x = [
-        remote(0, zone.at[2:4], zone.at[34:36], 8),
-        remote(1, zone.at[32:34], zone.at[0:2], 9),
-    ]
-    start(zone_x)
+    def push(present, device, source, target, out_slot, in_slot):
+        @pl.when(present)
+        def _():
+            pltpu.make_async_remote_copy(
+                src_ref=source,
+                dst_ref=target,
+                send_sem=send_sem.at[out_slot],
+                recv_sem=recv_sem.at[in_slot],
+                device_id=device,
+                device_id_type=MESH,
+            ).start()
+
+    def pushed(present, source, slot):
+        @pl.when(present)
+        def _():
+            pltpu.make_async_copy(source, source, send_sem.at[slot]).wait()
+
+    def arrived(present, target, slot):
+        @pl.when(present)
+        def _():
+            pltpu.make_async_copy(target, target, recv_sem.at[slot]).wait()
+
+    for n in range(2):
+        push(*sides[n], r_own.at[:, 2 + 31 * n], r_own.at[:, 34 - 33 * n], n, 1 - n)
+    for c in range(4):
+        push(*sides[4 + c], r_corner_send.at[c], r_corner.at[3 - c], 4 + c, 7 - c)
+    for n in range(2):
+        push(*sides[2 + n], r_send.at[n], r_recv.at[1 - n], 2 + n, 3 - n)
+    for n in range(2):
+        push(*sides[n], zone.at[2 + 30 * n : 4 + 30 * n], zone.at[34 - 34 * n : 36 - 34 * n], 30 + n, 31 - n)
 
     table = [[ref[f, q] for q in range(ZONES)] for ref in (cond_ref, cap_ref) for f in range(2)]
     table.append([coup_ref[q] for q in range(ZONES)])
@@ -314,115 +295,116 @@
     lane_tail = lax.broadcasted_iota(jnp.int32, (1, 128), 1)
     low_lanes = jnp.logical_and(lane_tail >= 16, lane_tail < 32)
 
-    def apply_boxes(own, packed, out, out_pk):
-        for box in range(2):
-            columns = []
+    def apply_box(own, packed, out, out_pk, box):
+        layers = pl.ds(1 + BOX * box, SPAN)
+        spots = pl.ds(pl.multiple_of(BOX * box, 8), 24)
+        columns = []
+        for field in range(2):
+            inner = own[field, layers].reshape(OWN, NZ)
+            columns.append(jnp.concatenate([inner] + [packed[side, field, spots] for side in range(2)], axis=0))
+        high, low = halves(jnp.concatenate(columns, axis=1))
+        modes = dot(tf[...], jnp.concatenate([high, low, high], axis=0))
+        columns = []
+        for field in range(2):
+            high, low = halves(modes[:, NZ * field : NZ * (field + 1)])
+            deep = dot(jnp.concatenate([high, low, high], axis=1), zf[...])
+            deep = deep * dinv[2 * box + field]
+            high, low = halves(deep[:, :128])
+            tail = deep[:, 128:]
+            tail_high = tail.astype(BF16).astype(F32)
+            tail = jnp.where(low_lanes, tail - tail_high, tail_high).astype(BF16)
+            columns.append(dot(jnp.concatenate([high, low, high, tail], axis=1), zi[...]))
+        high, low = halves(jnp.concatenate(columns, axis=1))
+        cells = dot(ti[...], jnp.concatenate([high, low, high], axis=0))
+        for field in range(2):
+            mine = cells[:, NZ * field : NZ * (field + 1)]
+            out[field, layers] += mine[:OWN].reshape(SPAN, BY, NZ)
+            out_pk[:, field, spots] += mine[OWN:].reshape(6, 24, NZ)
+
+    def tile(side):
+        return pl.ds(pl.multiple_of(32 * side, 8), 4)
+
+    def x_messages(width, own, packed, bufs, base, side, present, side_gx, act):
+        x_layers, x_corner, x_corner_send, y_rows, corners, corners_send = bufs
+        layers = pl.ds(1 + (34 - width) * side, width)
+        device = (side_gx, gy)
+        if act == "push":
+            for place, row in enumerate((0, 5)):
+                x_corner_send[side, place] = packed[row, :, tile(side)]
+            push(present, device, own.at[:, layers], x_layers.at[1 - side], base + side, base + 1 - side)
+            push(present, device, x_corner_send.at[side], x_corner.at[1 - side], base + 8 + side, base + 9 - side)
+        elif act == "pushed":
+            pushed(present, own.at[:, layers], base + side)
+            pushed(present, x_corner_send.at[side], base + 8 + side)
+        else:
+            arrived(present, x_layers.at[side], base + side)
+            arrived(present, x_corner.at[side], base + 8 + side)
+        for n in range(2):
+            c = 2 * side + n
+            both = jnp.logical_and(present, y_here[n])
+            if act == "push":
+                for place in range(width):
+                    corners_send[c, place] = packed[(6 - width) * n + place, :, tile(side)]
+                device = (side_gx, gy - 1 + 2 * n)
+                push(both, device, corners_send.at[c], corners.at[3 - c], base + 4 + c, base + 7 - c)
+            elif act == "pushed":
+                pushed(both, corners_send.at[c], base + 4 + c)
+            else:
+                arrived(both, corners.at[c], base + 4 + c)
+
+    def y_messages(width, packed, bufs, base, act):
+        y_rows = bufs[3]
+        for n in range(2):
+            rows = packed.at[(6 - width) * n : (6 - width) * n + width]
+            if act == "push":
+                push(*sides[2 + n], rows, y_rows.at[1 - n], base + 2 + n, base + 3 - n)
+            elif act == "pushed":
+                pushed(y_here[n], rows, base + 2 + n)
+            else:
+                arrived(y_here[n], y_rows.at[n], base + 2 + n)
+
+    rows_pk = lax.broadcasted_iota(jnp.int32, (PX, NZ), 0)
+
+    def corner_rows(side):
+        for n in range(2):
             for field in range(2):
-                inner = own[field, 1 + BOX * box : 1 + BOX * box + SPAN].reshape(OWN, NZ)
-                edge = [packed[side, field, BOX * box : BOX * box + 24] for side in range(2)]
-                columns.append(jnp.concatenate([inner] + edge, axis=0))
-            high, low = halves(jnp.concatenate(columns, axis=1))
-            modes = dot(tf[...], jnp.concatenate([high, low, high], axis=0))
-            columns = []
-            for field in range(2):
-                high, low = halves(modes[:, NZ * field : NZ * (field + 1)])
-                deep = dot(jnp.concatenate([high, low, high], axis=1), zf[...])
-                deep = deep * dinv[2 * box + field]
-                high, low = halves(deep[:, :128])
-                tail = deep[:, 128:]
-                tail_high = tail.astype(BF16).astype(F32)
-                tail = jnp.where(low_lanes, tail - tail_high, tail_high).astype(BF16)
-                columns.append(dot(jnp.concatenate([high, low, high, tail], axis=1), zi[...]))
-            high, low = halves(jnp.concatenate(columns, axis=1))
-            cells = dot(ti[...], jnp.concatenate([high, low, high], axis=0))
-            for field in range(2):
-                mine = cells[:, NZ * field : NZ * (field + 1)]
-                inner = mine[:OWN].reshape(SPAN, BY, NZ)
-                edge = mine[OWN:].reshape(6, 24, NZ)
-                if box == 0:
-                    out[field, 1:19] = inner
-                    out_pk[:, field, 0:24] = edge
-                else:
-                    out[field, 17:19] += inner[:2]
-                    out[field, 19:35] = inner[2:]
-                    out_pk[:, field, 16:24] += edge[:, :8]
-                    out_pk[:, field, 24:40] = edge[:, 8:]
-
-    for (present, copy), number in zip(first, origin):
-
-        @pl.when(sides[number][1])
-        def _():
-            copy.wait_recv()
-
-    for side in range(2):
-        for field in range(2):
-            r_pk[side, field, 2:34] = r_recv[side, field]
-    for corner, (side, spot) in enumerate(((0, 1), (1, 34), (1, 1), (0, 34))):
-        for field in range(2):
-            r_pk[side, field, spot : spot + 1] = r_corner[corner, field : field + 1]
-    apply_boxes(r_own, r_pk, u1, p1)
-    finish_send(first)
-
-    def exchange(width, own, packed, x_layers, x_corner, x_corner_send, y_rows, corners, corners_send, slot):
-        low_layer = 1
-        high_layer = 35 - width
-        rows_low = packed.at[0:width]
-        rows_high = packed.at[6 - width : 6]
-        for side in range(2):
-            for place, row in enumerate((0, 5)):
-                x_corner_send[side, place] = packed[row, :, 32 * side : 32 * side + 4]
-        for corner, (x_side, y_side) in enumerate(((0, 0), (1, 1), (0, 1), (1, 0))):
-            start_row = (6 - width) * y_side
-            for place in range(width):
-                corners_send[corner, place] = packed[start_row + place, :, 32 * x_side : 32 * x_side + 4]
-        return [
-            remote(0, own.at[:, low_layer : low_layer + width], x_layers.at[1], slot),
-            remote(1, own.at[:, high_layer : high_layer + width], x_layers.at[0], slot + 1),
-            remote(2, rows_low, y_rows.at[1], slot + 2),
-            remote(3, rows_high, y_rows.at[0], slot + 3),
-            remote(4, corners_send.at[0], corners.at[1], slot + 4),
-            remote(5, corners_send.at[1], corners.at[0], slot + 5),
-            remote(6, corners_send.at[2], corners.at[3], slot + 6),
-            remote(7, corners_send.at[3], corners.at[2], slot + 7),
-            remote(0, x_corner_send.at[0], x_corner.at[1], slot + 8),
-            remote(1, x_corner_send.at[1], x_corner.at[0], slot + 9),
-        ]
-
-    origin10 = origin + [1, 0]
-
-    def start_far_first(copies):
-        along_y = copies[2:4]
-        others = copies[:2] + copies[8:] + copies[4:8]
-        start(others)
-        finish_send(others)
-        start(along_y)
-
-    second = exchange(3, u1, p1, xl1, xc1, xcs1, yr1, dg1, dgs1, 12)
-    start_far_first(second)
-
-    for (present, copy), number in zip(zone_x, origin[:2]):
-
-        @pl.when(sides[number][1])
-        def _():
-            copy.wait_recv()
-
-    finish_send(zone_x)
-    for side, name in enumerate(("xm", "xp")):
-
-        @pl.when(jnp.logical_not(has[name]))
-        def _():
-            edge = zone[2 + 31 * side]
-            zone[34 * side] = edge
-            zone[34 * side + 1] = edge
+                row = r_corner[2 * side + n, field : field + 1]
+                r_pk[n, field] = jnp.where(rows_pk == 1 + 33 * side, row, r_pk[n, field])
+
+    for n in range(2):
+        arrived(y_here[n], r_recv.at[n], 2 + n)
+        for field in range(2):
+            r_pk[n, field, 2:34] = r_recv[n, field]
+        arrived(jnp.logical_and(near_here, y_here[n]), r_corner.at[2 * near + n], 4 + 2 * near + n)
+    arrived(near_here, r_own.at[:, 1 + 33 * near], near)
+    corner_rows(near)
+    set1 = (xl1, xc1, xcs1, yr1, dg1, dgs1)
+    set2 = (xl2, xc2, xcs2, yr2, dg2, dgs2)
+    apply_box(r_own, r_pk, u1, p1, near)
+    x_messages(3, u1, p1, set1, 10, near, near_here, near_gx, "push")
+    for n in range(2):
+        arrived(jnp.logical_and(late_here, y_here[n]), r_corner.at[2 * late + n], 4 + 2 * late + n)
+    arrived(late_here, r_own.at[:, 1 + 33 * late], late)
+    corner_rows(late)
+    apply_box(r_own, r_pk, u1, p1, late)
+    x_messages(3, u1, p1, set1, 10, late, late_here, late_gx, "push")
+
+    for n in range(2):
+        arrived(sides[n][0], zone.at[34 * n : 34 * n + 2], 30 + n)
+
+        @pl.when(jnp.logical_not(sides[n][0]))
+        def _():
+            edge = zone[2 + 31 * n]
+            zone[34 * n] = edge
+            zone[34 * n + 1] = edge
 
     for place, row in enumerate((0, 1, 14, 15)):
         zone_send[place] = jnp.zeros((PX, NZ), jnp.int32)
         zone_send[place, 0:LX] = zone[:, row]
-    zone_y = [
-        remote(2, zone_send.at[0:2], zone_recv.at[1], 10),
-        remote(3, zone_send.at[2:4], zone_recv.at[0], 11),
-    ]
-    start(zone_y)
+    for n in range(2):
+        push(*sides[2 + n], zone_send.at[2 * n : 2 * n + 2], zone_recv.at[1 - n], 32 + n, 33 - n)
+    x_messages(3, u1, p1, set1, 10, late, late_here, late_gx, "pushed")
+    y_messages(3, p1, set1, 10, "push")
     for layer in (0, 1, 34, 35):
         k0, k1, c0, c1, share = lookup(zone[layer], table)
         k_own[layer, 8:24] = k0
@@ -430,20 +412,14 @@
         c_own[0, layer] = c0
         c_own[1, layer] = c1
         cross[layer] = share * jnp.sqrt(c0 * c1)
-    for (present, copy), number in zip(zone_y, origin[2:4]):
-
-        @pl.when(sides[number][1])
-        def _():
-            copy.wait_recv()
-
-    finish_send(zone_y)
-    for side, name in enumerate(("ym", "yp")):
-
-        @pl.when(jnp.logical_not(has[name]))
-        def _():
-            edge = zone_send[3 * side]
-            zone_recv[side, 0] = edge
-            zone_recv[side, 1] = edge
+    for n in range(2):
+        arrived(y_here[n], zone_recv.at[n], 32 + n)
+
+        @pl.when(jnp.logical_not(y_here[n]))
+        def _():
+            edge = zone_send[3 * n]
+            zone_recv[n, 0] = edge
+            zone_recv[n, 1] = edge
 
     for place in range(6):
         packed_zone = (
@@ -492,7 +468,6 @@
 
     lanes_pk = lax.broadcasted_iota(jnp.int32, (PX, NZ), 1)
     first_pk, last_pk = lanes_pk == 0, lanes_pk == NZ - 1
-    rows_pk = lax.broadcasted_iota(jnp.int32, (PX, NZ), 0)
 
     def rim_faces(side, field):
         center = k_pk[1 + 3 * side, field]
@@ -504,17 +479,9 @@
         z_high = 0.5 * (center + jnp.where(last_pk, center, pltpu.roll(center, NZ - 1, axis=1)))
         return x_low, x_high, y_low, y_high, z_low, z_high
 
-    def outside(value, present):
-        return jnp.where(present, value, 0.0)
-
-    for (present, copy), number in zip(second, origin10):
-
-        @pl.when(sides[number][1])
-        def _():
-            copy.wait_recv()
-
-    def assemble(width, own, packed, x_layers, x_corner, y_rows, corners, total_v, total_pk, margin):
-        low0, high0 = 3 - width, 33
+    def assemble_near(width, own, packed, bufs, total_v, total_pk, margin):
+        x_layers, x_corner, _, y_rows, corners, _ = bufs
+        low0 = 3 - width
         for field in range(2):
             base = LX * field
 
@@ -523,59 +490,64 @@
                 return carry
 
             lax.fori_loop(3, 33, copy_layer, 0, unroll=6)
+            for side, present in ((near, near_here), (late, late_here)):
+                for step in range(width):
+                    layer = low0 + (33 - low0) * side + step
+                    value = own[field, layer]
+                    if side is near:
+                        value = value + x_layers[near, field, step]
+                    beyond = jnp.logical_or(layer < 2, layer > 33)
+                    drop = jnp.logical_and(beyond, jnp.logical_not(present))
+                    total_v[base + layer, 8:24] = jnp.where(drop, 0.0, value)
+        low_x = jnp.logical_and(rows_pk < 2, jnp.logical_not(has["xm"]))
+        high_x = jnp.logical_and(rows_pk > 33, jnp.logical_not(has["xp"]))
+        beyond_x = jnp.logical_or(low_x, high_x)
+        for n in range(2):
             for step in range(width):
-                layer = low0 + step
-                value = x_layers[0, field, step]
-                if layer >= 1:
-                    value = value + own[field, layer]
-                if layer < 2:
-                    value = outside(value, has["xm"])
-                total_v[base + layer, 8:24] = value
-                layer = high0 + step
-                value = x_layers[1, field, step]
-                if layer <= 34:
-                    value = value + own[field, layer]
-                if layer > 33:
-                    value = outside(value, has["xp"])
-                total_v[base + layer, 8:24] = value
-        for side in range(2):
-            for step in range(width):
-                y = 1 - width + step if side == 0 else 15 + step
-                place = y + 2 if side == 0 else y - 12
-                total_pk[place] = y_rows[side, step]
-                minus, plus = (0, 3) if side == 0 else (2, 1)
-                total_pk[place, :, 0:4] += corners[minus, step]
-                total_pk[place, :, 32:36] += corners[plus, step]
+                y = 1 - width + step if n == 0 else 15 + step
+                place = y + 2 if n == 0 else y - 12
+                total_pk[place] = y_rows[n, step]
+                total_pk[place, :, tile(near)] += corners[2 * near + n, step]
                 if y == -1 or y == 16:
-                    total_pk[place] += packed[5 * side]
-                    total_pk[place, :, 0:4] += x_corner[0, side]
-                    total_pk[place, :, 32:36] += x_corner[1, side]
+                    total_pk[place] += packed[5 * n]
+                    total_pk[place, :, tile(near)] += x_corner[near, n]
+                drop = beyond_x
                 if y < 0 or y > 15:
-                    present = has["ym"] if side == 0 else has["yp"]
-                    low_x = jnp.logical_and(rows_pk < 2, jnp.logical_not(has["xm"]))
-                    high_x = jnp.logical_and(rows_pk > 33, jnp.logical_not(has["xp"]))
-                    drop = jnp.logical_or(jnp.logical_or(low_x, high_x), jnp.logical_not(present))
-                    for field in range(2):
-                        total_pk[place, field] = jnp.where(drop, 0.0, total_pk[place, field])
+                    drop = jnp.logical_or(drop, jnp.logical_not(y_here[n]))
+                for field in range(2):
+                    total_pk[place, field] = jnp.where(drop, 0.0, total_pk[place, field])
         for field in range(2):
             lo = 2 - margin
             count = BX + 2 * margin
-            for side, row, halo in ((0, 8, 7), (1, 23, 24)):
-                place = 2 if side == 0 else 3
-                window = slice(LX * field + lo, LX * field + lo + count)
-                added = total_pk[place, field, lo : lo + count]
-                spots = lax.broadcasted_iota(jnp.int32, (count, NZ), 0) + lo
-                low_x = jnp.logical_and(spots < 2, jnp.logical_not(has["xm"]))
-                high_x = jnp.logical_and(spots > 33, jnp.logical_not(has["xp"]))
-                added = jnp.where(jnp.logical_or(low_x, high_x), 0.0, added)
-                edge = total_v[window, row] + added
+            window = slice(LX * field + lo, LX * field + lo + count)
+            for place, outer, row, halo in ((2, 1, 8, 7), (3, 4, 23, 24)):
+                edge = total_v[window, row] + total_pk[place, field, lo : lo + count]
                 total_v[window, row] = edge
-                if margin > 1:
-                    total_pk[place, field, lo : lo + count] = edge
-                outer = 1 if side == 0 else 4
+                total_pk[place, field, lo : lo + count] = edge
                 total_v[window, halo] = total_pk[outer, field, lo : lo + count]
 
-    assemble(3, u1, p1, xl1, xc1, yr1, dg1, v1, zp, 2)
+    def assemble_late(width, bufs, total_v, total_pk):
+        x_layers, x_corner, _, _, corners, _ = bufs
+        low0 = 3 - width
+        for field in range(2):
+            for step in range(width):
+                spot = LX * field + low0 + (33 - low0) * late + step
+                total_v[spot, 8:24] += x_layers[late, field, step]
+            block = pl.ds(LX * field + 32 * late, 4)
+            for n, edge_place, outer, row, halo in ((0, 2, 1, 8, 7), (1, 3, 4, 23, 24)):
+                for step in range(width):
+                    y = 1 - width + step if n == 0 else 15 + step
+                    place = y + 2 if n == 0 else y - 12
+                    piece = corners[2 * late + n, step, field]
+                    if y == -1 or y == 16:
+                        piece = piece + jnp.where(y_here[n], x_corner[late, n, field], 0.0)
+                    if place == edge_place:
+                        edge = total_v[block, row] + piece
+                        total_v[block, row] = edge
+                        total_pk[place, field, tile(late)] = edge
+                    else:
+                        total_pk[place, field, tile(late)] += piece
+                total_v[block, halo] = total_pk[outer, field, tile(late)]
 
     def operate(vec, layer, field):
         spot = LX * field + layer
@@ -598,39 +570,52 @@
             pq = pq + fold(center * value)
         return rz, pq
 
-    rz, pq = lax.fori_loop(2, 34, first_image, (zero, zero), unroll=4)
-    for layer, name in ((1, "xm"), (34, "xp")):
+    def rim_layer(side, present):
+        layer = 1 + 33 * side
         for field in range(2):
             value, _ = operate(v1, layer, field)
-            q_own[field, layer] = outside(value, has[name])
-    for side, name in enumerate(("ym", "yp")):
-        center_place = 1 + 3 * side
-        for field in range(2):
-            x_low, x_high, y_low, y_high, z_low, z_high = rim_faces(side, field)
-            center = zp[center_place, field]
-            value = c_pk[side, field] + ((x_low + x_high) + (y_low + y_high) + (z_low + z_high))
-            value = value * center + cross_pk[side] * zp[center_place, 1 - field]
-            value = value - x_low * pltpu.roll(center, 1, axis=0) - x_high * pltpu.roll(center, PX - 1, axis=0)
-            value = value - y_low * zp[3 * side, field] - y_high * zp[3 * side + 2, field]
-            value = value - jnp.where(first_pk, 0.0, z_low) * pltpu.roll(center, 1, axis=1)
-            value = value - jnp.where(last_pk, 0.0, z_high) * pltpu.roll(center, NZ - 1, axis=1)
+            q_own[field, layer] = jnp.where(present, value, 0.0)
+
+    def rim_rows():
+        for side in range(2):
+            place = 1 + 3 * side
             low_x = jnp.logical_and(rows_pk < 2, jnp.logical_not(has["xm"]))
             high_x = jnp.logical_and(rows_pk > 33, jnp.logical_not(has["xp"]))
-            drop = jnp.logical_or(jnp.logical_or(low_x, high_x), jnp.logical_not(has[name]))
-            unused_rows = jnp.logical_or(rows_pk < 1, rows_pk > 34)
-            q_pk[side, field] = jnp.where(jnp.logical_or(drop, unused_rows), 0.0, value)
-
-    apply_boxes(q_own, q_pk, u2, p2)
-    third = exchange(2, u2, p2, xl2, xc2, xcs2, yr2, dg2, dgs2, 22)
-    start_far_first(third)
-    finish_send(second[2:4])
-    for (present, copy), number in zip(third, origin10):
-
-        @pl.when(sides[number][1])
-        def _():
-            copy.wait_recv()
-
-    assemble(2, u2, p2, xl2, xc2, yr2, dg2, v2, wp, 1)
+            drop = jnp.logical_or(jnp.logical_or(low_x, high_x), jnp.logical_not(y_here[side]))
+            drop = jnp.logical_or(drop, jnp.logical_or(rows_pk < 1, rows_pk > 34))
+            for field in range(2):
+                x_low, x_high, y_low, y_high, z_low, z_high = rim_faces(side, field)
+                center = zp[place, field]
+                value = c_pk[side, field] + ((x_low + x_high) + (y_low + y_high) + (z_low + z_high))
+                value = value * center + cross_pk[side] * zp[place, 1 - field]
+                value = value - x_low * pltpu.roll(center, 1, axis=0) - x_high * pltpu.roll(center, PX - 1, axis=0)
+                value = value - y_low * zp[3 * side, field] - y_high * zp[3 * side + 2, field]
+                value = value - jnp.where(first_pk, 0.0, z_low) * pltpu.roll(center, 1, axis=1)
+                value = value - jnp.where(last_pk, 0.0, z_high) * pltpu.roll(center, NZ - 1, axis=1)
+                q_pk[side, field] = jnp.where(drop, 0.0, value)
+
+    def inner_layers(step, carry, image):
+        return image(4 - 2 * late + step, carry)
+
+    x_messages(3, u1, p1, set1, 10, near, near_here, near_gx, "arrived")
+    y_messages(3, p1, set1, 10, "arrived")
+    assemble_near(3, u1, p1, set1, v1, zp, 2)
+    sums = lax.fori_loop(0, 30, functools.partial(inner_layers, image=first_image), (zero, zero), unroll=3)
+    rim_layer(near, near_here)
+    rim_rows()
+    apply_box(q_own, q_pk, u2, p2, near)
+    x_messages(2, u2, p2, set2, 20, near, near_here, near_gx, "push")
+    x_messages(3, u1, p1, set1, 10, late, late_here, late_gx, "arrived")
+    assemble_late(3, set1, v1, zp)
+    for step in range(2):
+        sums = first_image(2 + 30 * late + step, sums)
+    rz, pq = sums
+    rim_layer(late, late_here)
+    rim_rows()
+    apply_box(q_own, q_pk, u2, p2, late)
+    x_messages(2, u2, p2, set2, 20, late, late_here, late_gx, "push")
+    x_messages(2, u2, p2, set2, 20, late, late_here, late_gx, "pushed")
+    y_messages(2, p2, set2, 20, "push")
 
     def second_image(layer, carry):
         rw, qw, zu, wu = carry
@@ -643,8 +628,26 @@
             wu = wu + fold(center * value)
         return rw, qw, zu, wu
 
-    rw, qw, zu, wu = lax.fori_loop(2, 34, second_image, (zero,) * 4, unroll=4)
-    finish_send(third[2:4])
+    x_messages(2, u2, p2, set2, 20, near, near_here, near_gx, "arrived")
+    y_messages(2, p2, set2, 20, "arrived")
+    assemble_near(2, u2, p2, set2, v2, wp, 1)
+    sums = lax.fori_loop(0, 30, functools.partial(inner_layers, image=second_image), (zero,) * 4, unroll=3)
+    for n in range(2):
+        pushed(sides[n][0], r_own.at[:, 2 + 31 * n], n)
+        pushed(sides[n][0], zone.at[2 + 30 * n : 4 + 30 * n], 30 + n)
+        pushed(y_here[n], r_send.at[n], 2 + n)
+        pushed(y_here[n], zone_send.at[2 * n : 2 * n + 2], 32 + n)
+    for c in range(4):
+        pushed(sides[4 + c][0], r_corner_send.at[c], 4 + c)
+    x_messages(3, u1, p1, set1, 10, near, near_here, near_gx, "pushed")
+    y_messages(3, p1, set1, 10, "pushed")
+    x_messages(2, u2, p2, set2, 20, near, near_here, near_gx, "pushed")
+    y_messages(2, p2, set2, 20, "pushed")
+    x_messages(2, u2, p2, set2, 20, late, late_here, late_gx, "arrived")
+    assemble_late(2, set2, v2, wp)
+    for step in range(2):
+        sums = second_image(2 + 30 * late + step, sums)
+    rw, qw, zu, wu = sums
 
     spot = lax.broadcasted_iota(jnp.int32, (1, NZ), 1)
     row = jnp.zeros((1, NZ), F32)
@@ -726,7 +729,7 @@
         ]
     scratch += [
         vmem(plane, 1, NZ), vmem(depth, 1, NZ),
-        pltpu.SemaphoreType.DMA((12,)), pltpu.SemaphoreType.DMA((32,)), pltpu.SemaphoreType.DMA((32,)),
+        pltpu.SemaphoreType.DMA((12,)), pltpu.SemaphoreType.DMA((34,)), pltpu.SemaphoreType.DMA((34,)),
         pltpu.SemaphoreType.DMA((2,)), pltpu.SemaphoreType.DMA((2,)),
     ]
     any_spec = pl.BlockSpec(memory_space=pltpu.HBM)

time: 67.8 us -> 64.1 us (0.945)
  Pallas kernels: 65.5 us -> 61.8 us
    pallas_call x1, Pallas kernels: 65.5 us -> 61.8 us  [shards(): pl.pallas_call(functools.partial(body, nx, ny), out_shape=(shape, shape),...]
where the time goes in v3:
time: 64.1 us; the launch traced here: 64 us
  Pallas kernels  61.8 us (96%)
  local copies, waits for them, and re-layouts  1.59 us (2%)
    pallas_call x1, Pallas kernels, shards(): pl.pallas_call(functools.partial(body, nx, ny), out_shape=(shape, shape),...  61.8 us
    unnamed x2, local copies, waits for them, and re-layouts  1.59 us

profile of v3, /device:TPU:1, one launch (start us, length us, event | category | flops | bytes accessed | tf_op | source)
XLA Modules:
  0.0 64.0 jit_solution(7818395069514848596)
XLA Ops:
  0.6 61.8 %pcg.1 = (f32[2,32,16,128]{3,2,1,0:T(8,128)S(1)}, f32[2,32,16,128]{3,2,1,0:T(8,128)S(1)}) custom-call(f32[2,32,16,128]{3,2,1,0:T(8,128)} %load_ref.1, s32[32,16,128]{2,1,0:T(8,128)} %zones_ref.1, f32[2,8]{1,0:T(2,128)} %cond_hbm.1, f32[2,8]{1,0:T(2,128)} %cap_hbm.1, f32[8]{0:T(128)} %coup_hbm.1, bf16[336,1008]{1,0:T(8,128)(2,1)} %constant.12.clone.tf_hbm, ...), custom_call_target="tpu_custom_call" | custom-call | tf_op jit(solution)/shard_map/pcg/pallas_call | solution.py:738
  62.4 0.8 %copy.15 = f32[2,32,16,128]{3,2,1,0:T(8,128)} copy(f32[2,32,16,128]{3,2,1,0:T(8,128)S(1)} %get-tuple-element.4) | data formatting | bytes 1048576
  63.2 0.8 %copy.16 = f32[2,32,16,128]{3,2,1,0:T(8,128)} copy(f32[2,32,16,128]{3,2,1,0:T(8,128)S(1)} %get-tuple-element.5) | data formatting | bytes 1048576

commit v4 on v3

--- a/solution.py
+++ b/solution.py
@@ -112,13 +112,13 @@
     nx, ny,
     load_ref, zones_ref, cond_hbm, cap_hbm, coup_hbm,
     tf_hbm, ti_hbm, zf_hbm, zi_hbm, lam_hbm, group_hbm,
-    x_out, r_out,
+    z_out, w_out, q_out, u_out, by_z_out, by_w_out,
     cond_ref, cap_ref, coup_ref, tf, ti, zf, zi, lam, group,
     r_own, r_pk, zone, zone_pk, zone_send, zone_recv,
     r_send, r_recv, r_corner_send, r_corner,
     k_own, k_pk, c_own, c_pk, cross, cross_pk,
     fx, fym, fyp, fzm, fzp, diag, diag_pk, dinv,
-    u1, p1, v1, zp, q_own, q_pk, u2, p2, v2, wp, u_vec,
+    u1, p1, v1, zp, q_own, q_pk, u2, p2, v2, wp,
     xl1, xc1, xcs1, yr1, dg1, dgs1, xl2, xc2, xcs2, yr2, dg2, dgs2,
     ar1, ar2,
     local_sem, send_sem, recv_sem, ar_send, ar_recv,
@@ -168,9 +168,6 @@
             ((tf_hbm, tf), (zf_hbm, zf), (group_hbm, group), (lam_hbm, lam), (zi_hbm, zi), (ti_hbm, ti))
         )
     ]
-    for copy in loads + weights:
-        copy.start()
-
     barrier = pltpu.get_barrier_semaphore()
     for present, device in sides:
 
@@ -186,8 +183,10 @@
         pl.semaphore_signal(barrier, inc=1, device_id=depth_id(k), device_id_type=MESH)
         return carry
 
+    lax.fori_loop(1, depth, greet_depth, 0)
+    for copy in loads + weights:
+        copy.start()
     lax.fori_loop(1, plane, greet_plane, 0)
-    lax.fori_loop(1, depth, greet_depth, 0)
 
     def clear(*refs):
         for ref in refs:
@@ -290,7 +289,7 @@
         for field in range(2):
             cbar = means[4 * box + field : 4 * box + field + 1] + unused
             kbar = means[4 * box + 2 + field : 4 * box + 3 + field]
-            dinv[2 * box + field] = 1.0 / (cbar + kbar * lam[...])
+            dinv[box, MODES * field : MODES * (field + 1)] = 1.0 / (cbar + kbar * lam[...])
 
     lane_tail = lax.broadcasted_iota(jnp.int32, (1, 128), 1)
     low_lanes = jnp.logical_and(lane_tail >= 16, lane_tail < 32)
@@ -304,16 +303,14 @@
             columns.append(jnp.concatenate([inner] + [packed[side, field, spots] for side in range(2)], axis=0))
         high, low = halves(jnp.concatenate(columns, axis=1))
         modes = dot(tf[...], jnp.concatenate([high, low, high], axis=0))
-        columns = []
-        for field in range(2):
-            high, low = halves(modes[:, NZ * field : NZ * (field + 1)])
-            deep = dot(jnp.concatenate([high, low, high], axis=1), zf[...])
-            deep = deep * dinv[2 * box + field]
-            high, low = halves(deep[:, :128])
-            tail = deep[:, 128:]
-            tail_high = tail.astype(BF16).astype(F32)
-            tail = jnp.where(low_lanes, tail - tail_high, tail_high).astype(BF16)
-            columns.append(dot(jnp.concatenate([high, low, high, tail], axis=1), zi[...]))
+        high, low = halves(jnp.concatenate([modes[:, :NZ], modes[:, NZ:]], axis=0))
+        deep = dot(jnp.concatenate([high, low, high], axis=1), zf[...]) * dinv[box]
+        high, low = halves(deep[:, :128])
+        tail = deep[:, 128:]
+        tail_high = tail.astype(BF16).astype(F32)
+        tail = jnp.where(low_lanes, tail - tail_high, tail_high).astype(BF16)
+        lines = dot(jnp.concatenate([high, low, high, tail], axis=1), zi[...])
+        columns = [lines[:MODES], lines[MODES:]]
         high, low = halves(jnp.concatenate(columns, axis=1))
         cells = dot(ti[...], jnp.concatenate([high, low, high], axis=0))
         for field in range(2):
@@ -403,8 +400,8 @@
         zone_send[place, 0:LX] = zone[:, row]
     for n in range(2):
         push(*sides[2 + n], zone_send.at[2 * n : 2 * n + 2], zone_recv.at[1 - n], 32 + n, 33 - n)
+    y_messages(3, p1, set1, 10, "push")
     x_messages(3, u1, p1, set1, 10, late, late_here, late_gx, "pushed")
-    y_messages(3, p1, set1, 10, "push")
     for layer in (0, 1, 34, 35):
         k0, k1, c0, c1, share = lookup(zone[layer], table)
         k_own[layer, 8:24] = k0
@@ -566,6 +563,8 @@
         for field in range(2):
             value, center = operate(v1, layer, field)
             q_own[field, layer] = value
+            q_out[field, layer - 2] = value
+            z_out[field, layer - 2] = center
             rz = rz + fold(r_own[field, layer] * center)
             pq = pq + fold(center * value)
         return rz, pq
@@ -621,7 +620,8 @@
         rw, qw, zu, wu = carry
         for field in range(2):
             value, center = operate(v2, layer, field)
-            u_vec[field, layer] = value
+            u_out[field, layer - 2] = value
+            w_out[field, layer - 2] = center
             rw = rw + fold(r_own[field, layer] * center)
             qw = qw + fold(q_own[field, layer] * center)
             zu = zu + fold(v1[LX * field + layer, 8:24] * value)
@@ -649,10 +649,14 @@
         sums = second_image(2 + 30 * late + step, sums)
     rw, qw, zu, wu = sums
 
-    spot = lax.broadcasted_iota(jnp.int32, (1, NZ), 1)
-    row = jnp.zeros((1, NZ), F32)
-    for place, value in enumerate((rz, pq, rw, qw, zu, wu)):
-        row = jnp.where(spot == place, jnp.sum(value), row)
+    rows = [jnp.sum(v, axis=0, keepdims=True) for v in (rz, pq, rw, qw, zu, wu)]
+    stack = jnp.concatenate(rows + [jnp.zeros((2, NZ), F32)], axis=0)
+    for shift in (64, 32, 16):
+        stack = stack + pltpu.roll(stack, shift, axis=1)
+    group_of = lax.broadcasted_iota(jnp.int32, (8, NZ), 1) // 16
+    mine = group_of == lax.broadcasted_iota(jnp.int32, (8, NZ), 0)
+    spot = lax.broadcasted_iota(jnp.int32, (1, NZ), 1) // 16
+    row = jnp.sum(jnp.where(mine, stack, 0.0), axis=0, keepdims=True)
     ar1[0] = row
 
     def all_reduce(slots, count, device_of, number):
@@ -667,7 +671,7 @@
             ).start()
             return carry
 
-        for k in range(1, count):
+        for k in sorted(range(1, count), key=lambda k: -min(k, count - k)):
             send(k, 0)
         others = slots.at[1:count]
         pltpu.make_async_copy(others, others, ar_recv.at[number]).wait()
@@ -684,19 +688,8 @@
     grow = 1.0 + rz2 / rz
     curve = grow * grow * pq - grow * alpha * (zu + qw) + alpha * alpha * wu
     alpha2 = rz2 / curve
-    by_z = jnp.broadcast_to(alpha + alpha2 * grow, (BY, NZ))
-    by_w = jnp.broadcast_to(alpha2 * alpha, (BY, NZ))
-
-    def finish(layer, carry):
-        for field in range(2):
-            spot = LX * field + layer
-            x_out[field, layer - 2] = by_z * v1[spot, 8:24] - by_w * v2[spot, 8:24]
-            r_out[field, layer - 2] = (
-                r_own[field, layer] - by_z * q_own[field, layer] + by_w * u_vec[field, layer]
-            )
-        return carry
-
-    lax.fori_loop(2, 34, finish, 0, unroll=4)
+    by_z_out[...] = jnp.broadcast_to(alpha + alpha2 * grow, (1, NZ))
+    by_w_out[...] = jnp.broadcast_to(alpha2 * alpha, (1, NZ))
 
 
 def shards(nx, ny, load, zones, conductance, capacity, coupling):
@@ -716,11 +709,10 @@
         vmem(2 * LX, 32, NZ), vmem(6, 2, PX, NZ), vmem(2, LX, BY, NZ), vmem(2, 2, PX, NZ),
         vmem(LX, BY, NZ), vmem(2, PX, NZ),
         vmem(2, LX, BY, NZ), vmem(2, LX, BY, NZ), vmem(2, LX, BY, NZ), vmem(2, LX, BY, NZ),
-        vmem(2, LX, BY, NZ), vmem(2, LX, BY, NZ), vmem(8, NZ), vmem(4, MODES, 256),
+        vmem(2, LX, BY, NZ), vmem(2, LX, BY, NZ), vmem(8, NZ), vmem(2, 2 * MODES, 256),
         vmem(2, LX, BY, NZ), vmem(6, 2, PX, NZ), vmem(2 * LX, 32, NZ), vmem(6, 2, PX, NZ),
         vmem(2, LX, BY, NZ), vmem(2, 2, PX, NZ),
         vmem(2, LX, BY, NZ), vmem(6, 2, PX, NZ), vmem(2 * LX, 32, NZ), vmem(6, 2, PX, NZ),
-        vmem(2, LX, BY, NZ),
     ]
     for width in (3, 2):
         scratch += [
@@ -735,11 +727,11 @@
     any_spec = pl.BlockSpec(memory_space=pltpu.HBM)
     out = pl.BlockSpec(memory_space=pltpu.VMEM)
     shape = jax.ShapeDtypeStruct((2, BX, BY, NZ), F32)
-    return pl.pallas_call(
+    z1, w, q1, u, by_z, by_w = pl.pallas_call(
         functools.partial(body, nx, ny),
-        out_shape=(shape, shape),
+        out_shape=(shape,) * 4 + (jax.ShapeDtypeStruct((1, NZ), F32),) * 2,
         in_specs=[any_spec] * 11,
-        out_specs=(out, out),
+        out_specs=(out,) * 6,
         scratch_shapes=scratch,
         compiler_params=pltpu.CompilerParams(
             collective_id=0, has_side_effects=True, vmem_limit_bytes=48 * 1024 * 1024
@@ -749,6 +741,8 @@
         *(pltpu.with_memory_space_constraint(a, pltpu.HBM) for a in (load, zones, conductance, capacity, coupling)),
         *(pltpu.with_memory_space_constraint(jnp.asarray(c), pltpu.HBM) for c in (to_modes, from_modes, z_forward, z_inverse, summed, group)),
     )
+    by_z, by_w = by_z.reshape(NZ), by_w.reshape(NZ)
+    return by_z * z1 - by_w * w, load - by_z * q1 + by_w * u
 
 
 def solution(mesh):

time: 64.1 us -> 63.6 us (level)
  local copies, waits for them, and re-layouts: 1.59 us -> 0.01 us
  other arithmetic: 0 us -> 1.2 us
    unnamed x2, local copies, waits for them, and re-layouts: 1.59 us -> 0.01 us
    add x0 -> x1, other arithmetic: none -> 1.2 us  [shards(): return (by_z * z1 - by_w * w, load - by_z * q1 + by_w * u)]
where the time goes in v4:
time: 63.6 us; the launch traced here: 63.5 us
  Pallas kernels  61.6 us (97%)
  other arithmetic  1.2 us (2%)
  between operations  0.65 us (1%)
    pallas_call x1, Pallas kernels, shards(): pl.pallas_call(functools.partial(body, nx, ny), out_shape=(shape,) * 4 +...  61.6 us

profile of v4, /device:TPU:1, one launch (start us, length us, event | category | flops | bytes accessed | tf_op | source)
XLA Modules:
  0.0 63.5 jit_solution(12248513619296319846)
XLA Ops:
  0.6 0.0 copy-start
  0.6 61.6 %pcg.1 = (f32[2,32,16,128]{3,2,1,0:T(8,128)S(1)}, f32[2,32,16,128]{3,2,1,0:T(8,128)S(1)}, f32[2,32,16,128]{3,2,1,0:T(8,128)S(1)}, f32[2,32,16,128]{3,2,1,0:T(8,1...) custom-call(f32[2,32,16,128]{3,2,1,0:T(8,128)} %load_ref.1, s32[32,16,128]{2,1,0:T(8,128)} %zones_ref.1, ...), custom_call_target="tpu_custom_call" | custom-call | tf_op jit(solution)/shard_map/pcg/pallas_call | solution.py:730
  62.3 0.0 copy-done
  62.3 1.2 %multiply_add_fusion = (f32[2,32,16,128]{3,2,1,0:T(8,128)}, f32[2,32,16,128]{3,2,1,0:T(8,128)}) fusion(f32[2,32,16,128]{3,2,1,0:T(8,128)S(1)} %get-tuple-element.13, f32[2,32,16,128]{3,2,1,0:T(8,128)S(1)} %copy-done, f32[2,32,16,128]{3,2,1,0:T(8,128)S(1)} %get-tuple-element.12, f32[128]{0:T(128)S(1)} %bitcast.3, f32[128]{0:T(128)S(1)} %bitcast.2, ...), kind=kLoop, calls=%fused_computation | loop fusion | flops 917504 | bytes 3671040 | tf_op jit(solution)/shard_map/add | solution.py:745
Async XLA Ops:
  0.6 61.6 %copy-start = (f32[2,32,16,128]{3,2,1,0:T(8,128)S(1)}, f32[2,32,16,128]{3,2,1,0:T(8,128)}, u32[]{:S(2)}) copy-start(f32[2,32,16,128]{3,2,1,0:T(8,128)} %load_ref.1) | copy-start | bytes 1572868

commit v5 on v4

--- a/solution.py
+++ b/solution.py
@@ -120,7 +120,7 @@
     fx, fym, fyp, fzm, fzp, diag, diag_pk, dinv,
     u1, p1, v1, zp, q_own, q_pk, u2, p2, v2, wp,
     xl1, xc1, xcs1, yr1, dg1, dgs1, xl2, xc2, xcs2, yr2, dg2, dgs2,
-    ar1, ar2,
+    rim, ar1, ar2,
     local_sem, send_sem, recv_sem, ar_send, ar_recv,
 ):
     gx = lax.axis_index("gx")
@@ -326,9 +326,9 @@
         layers = pl.ds(1 + (34 - width) * side, width)
         device = (side_gx, gy)
         if act == "push":
+            push(present, device, own.at[:, layers], x_layers.at[1 - side], base + side, base + 1 - side)
             for place, row in enumerate((0, 5)):
                 x_corner_send[side, place] = packed[row, :, tile(side)]
-            push(present, device, own.at[:, layers], x_layers.at[1 - side], base + side, base + 1 - side)
             push(present, device, x_corner_send.at[side], x_corner.at[1 - side], base + 8 + side, base + 9 - side)
         elif act == "pushed":
             pushed(present, own.at[:, layers], base + side)
@@ -475,6 +475,18 @@
         z_low = 0.5 * (center + jnp.where(first_pk, center, pltpu.roll(center, 1, axis=1)))
         z_high = 0.5 * (center + jnp.where(last_pk, center, pltpu.roll(center, NZ - 1, axis=1)))
         return x_low, x_high, y_low, y_high, z_low, z_high
+
+    for side in range(2):
+        for field in range(2):
+            values = rim_faces(side, field)
+            x_low, x_high, y_low, y_high, z_low, z_high = values
+            for place, value in enumerate(values[:4]):
+                rim[side, field, place] = value
+            rim[side, field, 4] = jnp.where(first_pk, 0.0, z_low)
+            rim[side, field, 5] = jnp.where(last_pk, 0.0, z_high)
+            rim[side, field, 6] = c_pk[side, field] + (
+                (x_low + x_high) + (y_low + y_high) + (z_low + z_high)
+            )
 
     def assemble_near(width, own, packed, bufs, total_v, total_pk, margin):
         x_layers, x_corner, _, y_rows, corners, _ = bufs
@@ -583,14 +595,13 @@
             drop = jnp.logical_or(jnp.logical_or(low_x, high_x), jnp.logical_not(y_here[side]))
             drop = jnp.logical_or(drop, jnp.logical_or(rows_pk < 1, rows_pk > 34))
             for field in range(2):
-                x_low, x_high, y_low, y_high, z_low, z_high = rim_faces(side, field)
+                x_low, x_high, y_low, y_high, z_low, z_high, main = (rim[side, field, n] for n in range(7))
                 center = zp[place, field]
-                value = c_pk[side, field] + ((x_low + x_high) + (y_low + y_high) + (z_low + z_high))
-                value = value * center + cross_pk[side] * zp[place, 1 - field]
+                value = main * center + cross_pk[side] * zp[place, 1 - field]
                 value = value - x_low * pltpu.roll(center, 1, axis=0) - x_high * pltpu.roll(center, PX - 1, axis=0)
                 value = value - y_low * zp[3 * side, field] - y_high * zp[3 * side + 2, field]
-                value = value - jnp.where(first_pk, 0.0, z_low) * pltpu.roll(center, 1, axis=1)
-                value = value - jnp.where(last_pk, 0.0, z_high) * pltpu.roll(center, NZ - 1, axis=1)
+                value = value - z_low * pltpu.roll(center, 1, axis=1)
+                value = value - z_high * pltpu.roll(center, NZ - 1, axis=1)
                 q_pk[side, field] = jnp.where(drop, 0.0, value)
 
     def inner_layers(step, carry, image):
@@ -675,11 +686,13 @@
             send(k, 0)
         others = slots.at[1:count]
         pltpu.make_async_copy(others, others, ar_recv.at[number]).wait()
-        pltpu.make_async_copy(others, others, ar_send.at[number]).wait()
         return jnp.sum(slots[...], axis=0)
 
     ar2[0] = all_reduce(ar1, plane, plane_id, 0)
     products = all_reduce(ar2, depth, depth_id, 1)
+    for slots, count, number in ((ar1, plane, 0), (ar2, depth, 1)):
+        sent = slots.at[1:count]
+        pltpu.make_async_copy(sent, sent, ar_send.at[number]).wait()
     rz, pq, rw, qw, zu, wu = (
         jnp.sum(jnp.where(spot == n, products, 0.0), axis=1, keepdims=True) for n in range(6)
     )
@@ -720,7 +733,7 @@
             vmem(2, width, 2, PX, NZ), vmem(4, width, 2, 4, NZ), vmem(4, width, 2, 4, NZ),
         ]
     scratch += [
-        vmem(plane, 1, NZ), vmem(depth, 1, NZ),
+        vmem(2, 2, 7, PX, NZ), vmem(plane, 1, NZ), vmem(depth, 1, NZ),
         pltpu.SemaphoreType.DMA((12,)), pltpu.SemaphoreType.DMA((34,)), pltpu.SemaphoreType.DMA((34,)),
         pltpu.SemaphoreType.DMA((2,)), pltpu.SemaphoreType.DMA((2,)),
     ]

time: 63.6 us -> 63.6 us (level)
  no operation moved by 1% of the time
where the time goes in v5:
time: 63.6 us; the launch traced here: 63.5 us
  Pallas kernels  61.6 us (97%)
  other arithmetic  1.2 us (2%)
  between operations  0.65 us (1%)
    pallas_call x1, Pallas kernels, shards(): pl.pallas_call(functools.partial(body, nx, ny), out_shape=(shape,) * 4 +...  61.6 us

profile of v5, /device:TPU:1, one launch (start us, length us, event | category | flops | bytes accessed | tf_op | source)
XLA Modules:
  0.0 63.5 jit_solution(18320732219577918758)
XLA Ops:
  0.6 0.0 copy-start
  0.6 61.6 %pcg.1 = (f32[2,32,16,128]{3,2,1,0:T(8,128)S(1)}, f32[2,32,16,128]{3,2,1,0:T(8,128)S(1)}, f32[2,32,16,128]{3,2,1,0:T(8,128)S(1)}, f32[2,32,16,128]{3,2,1,0:T(8,1...) custom-call(f32[2,32,16,128]{3,2,1,0:T(8,128)} %load_ref.1, s32[32,16,128]{2,1,0:T(8,128)} %zones_ref.1, ...), custom_call_target="tpu_custom_call" | custom-call | tf_op jit(solution)/shard_map/pcg/pallas_call | solution.py:743
  62.2 0.0 copy-done
  62.3 1.2 %multiply_add_fusion = (f32[2,32,16,128]{3,2,1,0:T(8,128)}, f32[2,32,16,128]{3,2,1,0:T(8,128)}) fusion(f32[2,32,16,128]{3,2,1,0:T(8,128)S(1)} %get-tuple-element.13, f32[2,32,16,128]{3,2,1,0:T(8,128)S(1)} %copy-done, f32[2,32,16,128]{3,2,1,0:T(8,128)S(1)} %get-tuple-element.12, f32[128]{0:T(128)S(1)} %bitcast.3, f32[128]{0:T(128)S(1)} %bitcast.2, ...), kind=kLoop, calls=%fused_computation | loop fusion | flops 917504 | bytes 3671040 | tf_op jit(solution)/shard_map/add | solution.py:758
Async XLA Ops:
  0.6 61.6 %copy-start = (f32[2,32,16,128]{3,2,1,0:T(8,128)S(1)}, f32[2,32,16,128]{3,2,1,0:T(8,128)}, u32[]{:S(2)}) copy-start(f32[2,32,16,128]{3,2,1,0:T(8,128)} %load_ref.1) | copy-start | bytes 1572868

commit v6 on v4

--- a/solution.py
+++ b/solution.py
@@ -671,7 +671,8 @@
             ).start()
             return carry
 
-        for k in sorted(range(1, count), key=lambda k: -min(k, count - k)):
+        far_first = sorted(range(1, count), key=lambda k: -min(k, count - k))
+        for k in far_first if number == 1 else range(count - 1, 0, -1):
             send(k, 0)
         others = slots.at[1:count]
         pltpu.make_async_copy(others, others, ar_recv.at[number]).wait()

time: 63.6 us -> 63.6 us (level)
  no operation moved by 1% of the time
where the time goes in v6:
time: 63.6 us; the launch traced here: 63.5 us
  Pallas kernels  61.6 us (97%)
  other arithmetic  1.2 us (2%)
  between operations  0.65 us (1%)
    pallas_call x1, Pallas kernels, shards(): pl.pallas_call(functools.partial(body, nx, ny), out_shape=(shape,) * 4 +...  61.6 us

profile of v6, /device:TPU:1, one launch (start us, length us, event | category | flops | bytes accessed | tf_op | source)
XLA Modules:
  0.0 63.5 jit_solution(7268236365025581934)
XLA Ops:
  0.6 0.0 copy-start
  0.6 61.6 %pcg.1 = (f32[2,32,16,128]{3,2,1,0:T(8,128)S(1)}, f32[2,32,16,128]{3,2,1,0:T(8,128)S(1)}, f32[2,32,16,128]{3,2,1,0:T(8,128)S(1)}, f32[2,32,16,128]{3,2,1,0:T(8,1...) custom-call(f32[2,32,16,128]{3,2,1,0:T(8,128)} %load_ref.1, s32[32,16,128]{2,1,0:T(8,128)} %zones_ref.1, ...), custom_call_target="tpu_custom_call" | custom-call | tf_op jit(solution)/shard_map/pcg/pallas_call | solution.py:731
  62.3 0.0 copy-done
  62.3 1.2 %multiply_add_fusion = (f32[2,32,16,128]{3,2,1,0:T(8,128)}, f32[2,32,16,128]{3,2,1,0:T(8,128)}) fusion(f32[2,32,16,128]{3,2,1,0:T(8,128)S(1)} %get-tuple-element.13, f32[2,32,16,128]{3,2,1,0:T(8,128)S(1)} %copy-done, f32[2,32,16,128]{3,2,1,0:T(8,128)S(1)} %get-tuple-element.12, f32[128]{0:T(128)S(1)} %bitcast.3, f32[128]{0:T(128)S(1)} %bitcast.2, ...), kind=kLoop, calls=%fused_computation | loop fusion | flops 917504 | bytes 3671040 | tf_op jit(solution)/shard_map/add | solution.py:746
Async XLA Ops:
  0.6 61.6 %copy-start = (f32[2,32,16,128]{3,2,1,0:T(8,128)S(1)}, f32[2,32,16,128]{3,2,1,0:T(8,128)}, u32[]{:S(2)}) copy-start(f32[2,32,16,128]{3,2,1,0:T(8,128)} %load_ref.1) | copy-start | bytes 1572868
